TPU v7x, 32 devices: a whole 2x2x4 slice. The times are simulated.
32 devices in a mesh: hid: 8 (over z, core), wid: 4 (over y, x).
Axes of the slice: x: 2, y: 2, z: 4, core: 2. Of those that a mesh axis runs over, the one named last changes fastest.
Arguments:
- grad_out: bfloat16 [64, 12288], P('hid', 'wid'), may hold values from -3 to 3
- pre_act: bfloat16 [64, 49152], P(None, 'hid'), may hold values from -6 to 6
- weight: bfloat16 [49152, 12288], P('hid', 'wid'), may hold values from -0.02734375 to 0.02734375
Outputs:
- grad_pre: bfloat16 [64, 49152], P('wid', 'hid')
- grad_weight: bfloat16 [49152, 12288], P('hid', 'wid')
All inputs are finite; a program needn't handle non-finite values.
Results may differ from a plain program's by a relative error of at most 0.0051.
Values may be sent and summed in bfloat16 or wider, within the bound.
No kernel may reach another device: no remote copies, remote signals or barrier semaphores. Data moves between devices by JAX's collectives and lax.ppermute only.
A program may use at most 128 MiB of HBM per device.

v0:
```python
import math

import jax
import jax.numpy as jnp
from jax import lax
from jax.sharding import PartitionSpec as P

coef = math.sqrt(2.0 / math.pi)


def gelu_parts(x):
    inner = coef * (x + 0.044715 * x * x * x)
    tangent = jnp.tanh(inner)
    value = 0.5 * x * (1.0 + tangent)
    slope = 0.5 * (1.0 + tangent) + 0.5 * x * (1.0 - tangent * tangent) * coef * (
        1.0 + 3.0 * 0.044715 * x * x
    )
    return (value, slope)


def contract_rows(left, right):
    return lax.dot_general(
        left, right, (((0,), (0,)), ((), ())), preferred_element_type=jnp.float32
    )


def contract_cols(left, right):
    return lax.dot_general(
        left, right, (((1,), (1,)), ((), ())), preferred_element_type=jnp.float32
    )


def local(grad_out, pre_act, weight):
    value, unused = gelu_parts(pre_act.astype(jnp.float32))
    hidden = value.astype(jnp.bfloat16)
    gathered = lax.all_gather(grad_out, "hid", axis=0, tiled=True)
    grad_w = contract_rows(hidden, gathered)
    partial_value = contract_cols(gathered, weight)
    share = lax.psum_scatter(partial_value, "wid", scatter_dimension=0, tiled=True)
    own_rows = share.shape[0]
    offset = lax.axis_index("wid") * own_rows
    local_pre = lax.dynamic_slice_in_dim(pre_act, offset, own_rows, 0)
    unused_value, slope = gelu_parts(local_pre.astype(jnp.float32))
    grad_pre = (share * slope).astype(jnp.bfloat16)
    return (grad_pre, grad_w.astype(jnp.bfloat16))


def solution(mesh):
    return jax.shard_map(
        local,
        mesh=mesh,
        in_specs=(P("hid", "wid"), P(None, "hid"), P("hid", "wid")),
        out_specs=(P("wid", "hid"), P("hid", "wid")),
        check_vma=False,
    )
```

profile of v0, /device:TPU:0, one launch (start us, length us, event | category | flops | bytes accessed | tf_op | source)
XLA Modules:
  0.0 83.0 jit_solution(14676352917141983411)
XLA Ops:
  7.2 0.0 reduce-scatter.2.cloned.1.call-start
  7.2 16.4 %all_gather.3 = bf16[64,3072]{1,0:T(8,128)(2,1)S(1)} all-gather(bf16[8,3072]{1,0:T(8,128)(2,1)} %param.3), channel_id=1, replica_groups=mesh['hid'=8,'wid'=4] {'hid'}, dimensions={0}, use_global_device_ids=true | all-gather | bytes 442368 | tf_op jit(solution)/shard_map/all_gather | solution.py:36
  23.7 18.2 %fusion.23 = f32[64,6144]{1,0:T(8,128)} fusion(bf16[64,3072]{1,0:T(8,128)(2,1)S(1)} %all_gather.3, bf16[6144,3072]{1,0:T(8,128)(2,1)} %param.5), kind=kOutput, calls=%fused_computation.35 | convolution fusion | flops 2415919104 | bytes 39714816 | tf_op jit(solution)/shard_map/dot_general | solution.py:28
  41.8 0.0 copy-start
  41.8 0.0 reduce-scatter.2.cloned.1.call-update
  41.9 1.1 %copy-done = bf16[64,6144]{1,0:T(8,128)(2,1)S(1)} copy-done((bf16[64,6144]{1,0:T(8,128)(2,1)S(1)}, bf16[64,6144]{1,0:T(8,128)(2,1)}, u32[]{:S(2)}) %copy-start) | copy-done | bytes 786456
  43.0 16.5 %convolution_convert_fusion = bf16[6144,3072]{1,0:T(8,128)(2,1)} fusion(bf16[64,3072]{1,0:T(8,128)(2,1)S(1)} %all_gather.3, bf16[64,6144]{1,0:T(8,128)(2,1)S(1)} %copy-done), kind=kOutput, calls=%fused_computation | convolution fusion | flops 2438725632 | bytes 38928384 | tf_op jit(solution)/shard_map/dot_general | solution.py:22
  59.5 14.7 %reduce-scatter.2.cloned.1.call-done = f32[16,6144]{1,0:T(8,128)} async-done(((f32[64,6144]{1,0:T(8,128)}), f32[16,6144]{1,0:T(8,128)}) %reduce-scatter.2.cloned.1.call-update) | async-done | bytes 393232 | tf_op jit(solution)/shard_map/reduce_scatter | solution.py:39
  74.2 1.9 %fusion.17 = bf16[16,6144]{1,0:T(8,128)(2,1)} fusion(f32[16,6144]{1,0:T(8,128)} %reduce-scatter.2.cloned.1.call-done, bf16[64,6144]{1,0:T(8,128)(2,1)S(1)} %copy-done, s32[]{:T(128)S(6)} %select_n.3), kind=kLoop, calls=%fused_computation.29 | loop fusion | flops 1966080 | bytes 786436 | tf_op jit(solution)/shard_map/convert_element_type | solution.py:44
Async XLA Ops:
  7.2 67.0 %reduce-scatter.2.cloned.1.call-start = ((), (), s32[]{:S(2)}) async-start(), calls=%async_computation.1 | async-start | bytes 1966080 | tf_op jit(solution)/shard_map/reduce_scatter | solution.py:39
  41.8 1.1 %copy-start = (bf16[64,6144]{1,0:T(8,128)(2,1)S(1)}, bf16[64,6144]{1,0:T(8,128)(2,1)}, u32[]{:S(2)}) copy-start(bf16[64,6144]{1,0:T(8,128)(2,1)} %param.4) | copy-start | bytes 2359300
Sparse Core Ops, SparseCore 0:
  42.0 32.1 reduce-scatter.1
where the time goes:
time: 83.2 us; the launch traced here: 83 us
  matrix products  34.7 us (42%)
  blocking collectives  16.4 us (20%)
  waiting for transfers between devices  14.7 us (18%)
  between operations  14 us (17%)
  other arithmetic  1.94 us (2%)
  local copies, waits for them, and re-layouts  1.1 us (1%)
    dot_general x1, matrix products, contract_cols(): lax.dot_general(left, right, (((1,), (1,)), ((), ())), preferred_element_...  18.2 us
    dot_general x1, matrix products, contract_rows(): lax.dot_general(left, right, (((0,), (0,)), ((), ())), preferred_element_...  16.5 us
    all_gather x1, blocking collectives, local(): gathered = lax.all_gather(grad_out, 'hid', axis=0, tiled=True)  16.4 us
    reduce_scatter x1, waiting for transfers between devices, local(): lax.psum_scatter(partial_value, 'wid', scatter_dimension=0, tiled=True)  14.7 us
    convert_element_type x1, other arithmetic, local(): grad_pre = (share * slope).astype(jnp.bfloat16)  1.94 us
  transfers between devices with their start and end apart: 1, of which 1 were waited for; matrix products, arithmetic and copies ran while one was open for 20% of the time, Pallas kernels for 0%

commit v1 on v0

v1 whole, which is shorter than its diff:
```python
import functools
import math

import jax
import jax.numpy as jnp
from jax import lax
from jax.experimental import pallas as pl
from jax.experimental.pallas import tpu as pltpu
from jax.sharding import PartitionSpec as P

coef = math.sqrt(2.0 / math.pi)
BF16 = jnp.bfloat16
F32 = jnp.float32


def gelu_parts(x):
    inner = coef * (x + 0.044715 * x * x * x)
    tangent = jnp.tanh(inner)
    value = 0.5 * x * (1.0 + tangent)
    slope = 0.5 * (1.0 + tangent) + 0.5 * x * (1.0 - tangent * tangent) * coef * (
        1.0 + 3.0 * 0.044715 * x * x
    )
    return (value, slope)


def contract_rows(left, right):
    return lax.dot_general(
        left, right, (((0,), (0,)), ((), ())), preferred_element_type=F32
    )


def contract_cols(left, right):
    return lax.dot_general(
        left, right, (((1,), (1,)), ((), ())), preferred_element_type=F32
    )


def plain(grad_out, pre_act, weight):
    value, unused = gelu_parts(pre_act.astype(F32))
    hidden = value.astype(BF16)
    gathered = lax.all_gather(grad_out, "hid", axis=0, tiled=True)
    grad_w = contract_rows(hidden, gathered)
    partial_value = contract_cols(gathered, weight)
    share = lax.psum_scatter(partial_value, "wid", scatter_dimension=0, tiled=True)
    own_rows = share.shape[0]
    offset = lax.axis_index("wid") * own_rows
    local_pre = lax.dynamic_slice_in_dim(pre_act, offset, own_rows, 0)
    unused_value, slope = gelu_parts(local_pre.astype(F32))
    grad_pre = (share * slope).astype(BF16)
    return (grad_pre, grad_w.astype(BF16))


VMEM = pltpu.VMEM


def in_vmem():
    return pl.BlockSpec(memory_space=pltpu.VMEM)


def anywhere():
    return pl.BlockSpec(memory_space=pl.ANY)


def params(mib):
    return pltpu.CompilerParams(vmem_limit_bytes=mib * 1024 * 1024)


def gelu_kernel(parts, x_ref, hidden_ref, slope_ref):
    own = lax.axis_index("wid")
    rows = x_ref.shape[0] // parts
    for b in range(parts):
        start = pl.multiple_of(lax.bitwise_xor(own, b) * rows, rows)
        x = x_ref[pl.ds(start, rows), :].astype(F32)
        value, slope = gelu_parts(x)
        hidden_ref[b * rows : (b + 1) * rows, :] = value.astype(BF16)
        if b == 0:
            slope_ref[...] = slope


def gelu_call(parts, x):
    tokens, width = x.shape
    return pl.pallas_call(
        functools.partial(gelu_kernel, parts),
        out_shape=(
            jax.ShapeDtypeStruct((tokens, width), BF16),
            jax.ShapeDtypeStruct((tokens // parts, width), F32),
        ),
        in_specs=[in_vmem()],
        out_specs=(in_vmem(), in_vmem()),
        compiler_params=params(8),
        cost_estimate=pl.CostEstimate(
            flops=tokens * width * 20, transcendentals=tokens * width, bytes_accessed=4 * tokens * width
        ),
        name="gelu",
    )(x)


def hidden_grad_kernel(n, parts, chunks, *refs):
    own_ref, swap_ref, far_ref, farswap_ref, w_ref = refs[:5]
    g_out, own_out = refs[5:7]
    sends = refs[7 : 7 + parts - 1]
    w_buf, g_buf, sems = refs[7 + parts - 1 :]
    chunk = w_ref.shape[0] // chunks
    copies = [
        pltpu.make_async_copy(
            w_ref.at[pl.ds(i * chunk, chunk)], w_buf.at[pl.ds(i * chunk, chunk)], sems.at[i]
        )
        for i in range(chunks)
    ]
    for copy in copies:
        copy.start()
    hid = lax.axis_index("hid")
    wid = lax.axis_index("wid")
    rows = own_ref.shape[0]
    per = n // parts

    def place(source):
        block = lax.bitwise_xor(source // per, wid)
        return block * per + lax.rem(source, per)

    g_buf[place(hid)] = own_ref[...]
    g_buf[place(lax.bitwise_xor(hid, 1))] = swap_ref[...]
    for j in range(n // 2 - 1):
        k = 2 * (j + 1)
        g_buf[place(lax.bitwise_xor(hid, k))] = far_ref[j * rows : (j + 1) * rows]
        g_buf[place(lax.bitwise_xor(hid, k ^ 1))] = farswap_ref[j * rows : (j + 1) * rows]
    g = g_buf[...].reshape(n * rows, own_ref.shape[1])
    g_out[...] = g
    share = n * rows // parts
    for i, copy in enumerate(copies):
        copy.wait()
        part = contract_cols(w_buf[i * chunk : (i + 1) * chunk], g).T
        columns = slice(i * chunk, (i + 1) * chunk)
        own_out[:, columns] = part[:share]
        for k in range(1, parts):
            sends[k - 1][:, columns] = part[k * share : (k + 1) * share].astype(BF16)


def hidden_grad_call(n, parts, chunks, own, swap, far, farswap, weight):
    rows, width = own.shape
    ff = weight.shape[0]
    tokens = n * rows
    share = tokens // parts
    return pl.pallas_call(
        functools.partial(hidden_grad_kernel, n, parts, chunks),
        out_shape=(
            jax.ShapeDtypeStruct((tokens, width), BF16),
            jax.ShapeDtypeStruct((share, ff), F32),
            *[jax.ShapeDtypeStruct((share, ff), BF16)] * (parts - 1),
        ),
        in_specs=[in_vmem()] * 4 + [anywhere()],
        out_specs=tuple([in_vmem()] * (parts + 1)),
        scratch_shapes=[
            VMEM((ff, width), BF16),
            VMEM((n, rows, width), BF16),
            pltpu.SemaphoreType.DMA((chunks,)),
        ],
        compiler_params=params(48),
        cost_estimate=pl.CostEstimate(
            flops=2 * tokens * width * ff, transcendentals=0, bytes_accessed=2 * width * ff
        ),
        name="hidden_grad",
    )(own, swap, far, farswap, weight)


def weight_grad_kernel(chunks, hidden_ref, g_ref, out_ref, buf, sems):
    chunk = out_ref.shape[0] // chunks
    copies = []
    for i in range(chunks):
        rows = pl.ds(i * chunk, chunk)
        buf[i * chunk : (i + 1) * chunk] = contract_rows(
            hidden_ref[:, i * chunk : (i + 1) * chunk], g_ref[...]
        ).astype(BF16)
        copy = pltpu.make_async_copy(buf.at[rows], out_ref.at[rows], sems.at[i])
        copy.start()
        copies.append(copy)
    for copy in copies:
        copy.wait()


def weight_grad_call(chunks, hidden, g):
    tokens, ff = hidden.shape
    width = g.shape[1]
    return pl.pallas_call(
        functools.partial(weight_grad_kernel, chunks),
        out_shape=jax.ShapeDtypeStruct((ff, width), BF16),
        in_specs=[in_vmem()] * 2,
        out_specs=anywhere(),
        scratch_shapes=[VMEM((ff, width), BF16), pltpu.SemaphoreType.DMA((chunks,))],
        compiler_params=params(48),
        cost_estimate=pl.CostEstimate(
            flops=2 * tokens * width * ff, transcendentals=0, bytes_accessed=2 * width * ff
        ),
        name="weight_grad",
    )(hidden, g)


def sum_kernel(own_ref, slope_ref, *refs):
    total = own_ref[...]
    for ref in refs[:-1]:
        total = total + ref[...].astype(F32)
    refs[-1][...] = (total * slope_ref[...]).astype(BF16)


def sum_call(own, slope, received):
    return pl.pallas_call(
        sum_kernel,
        out_shape=jax.ShapeDtypeStruct(own.shape, BF16),
        in_specs=[in_vmem()] * (2 + len(received)),
        out_specs=in_vmem(),
        compiler_params=params(8),
        name="total",
    )(own, slope, *received)


def ring(n, parts, chunks, grad_out, pre_act, weight):
    def swap(value, axis, size, k):
        return lax.ppermute(value, axis, [(i, i ^ k) for i in range(size)])

    own_swap = swap(grad_out, "hid", n, 1)
    far = [swap(grad_out, "hid", n, k) for k in range(2, n, 2)]
    hidden, slope = gelu_call(parts, pre_act)
    far = jnp.concatenate(far, axis=0)
    far_swap = swap(far, "hid", n, 1)
    g, own, *sends = hidden_grad_call(n, parts, chunks, grad_out, own_swap, far, far_swap, weight)
    received = [swap(s, "wid", parts, k + 1) for k, s in enumerate(sends)]
    grad_w = weight_grad_call(chunks, hidden, g)
    return (sum_call(own, slope, received), grad_w)


def power_of_two(size):
    return size & (size - 1) == 0


def solution(mesh):
    n, parts = mesh.shape["hid"], mesh.shape["wid"]

    def local(grad_out, pre_act, weight):
        ff, width = weight.shape
        chunk = 512
        small = power_of_two(n) and power_of_two(parts) and parts < n <= 8
        if small and ff % chunk == 0 and width % 256 == 0 and ff * width * 2 <= 40 * 2**20:
            return ring(n, parts, ff // chunk, grad_out, pre_act, weight)
        return plain(grad_out, pre_act, weight)

    return jax.shard_map(
        local,
        mesh=mesh,
        in_specs=(P("hid", "wid"), P(None, "hid"), P("hid", "wid")),
        out_specs=(P("wid", "hid"), P("hid", "wid")),
        check_vma=False,
    )
```

time: 83.2 us -> 57.2 us (0.69)
  Pallas kernels: 0 us -> 38.4 us
  matrix products: 34.7 us -> 0 us
  blocking collectives: 16.4 us -> 0 us
  between operations: 14 us -> 0.71 us
  starting transfers between devices: 0.04 us -> 9.77 us
  waiting for transfers between devices: 14.7 us -> 6.1 us
  other arithmetic: 1.94 us -> 0 us
  local copies, waits for them, and re-layouts: 1.1 us -> 1.94 us
    pallas_call x0 -> x4, Pallas kernels: none -> 38.4 us  [the longest x1 23.6 us: hidden_grad_call(): pl.pallas_call(functools.partial(hidden_grad_kernel, n, parts, chunks), o...]
    dot_general x2 -> x0, matrix products: 34.7 us -> none  [the longest x1 18.2 us: contract_cols(): lax.dot_general(left, right, (((1,), (1,)), ((), ())), preferred_element_...]
    all_gather x1 -> x0, blocking collectives: 16.4 us -> none  [local(): gathered = lax.all_gather(grad_out, 'hid', axis=0, tiled=True)]
    reduce_scatter x1 -> x0, waiting for transfers between devices: 14.7 us -> none  [local(): lax.psum_scatter(partial_value, 'wid', scatter_dimension=0, tiled=True)]
    ppermute x0 -> x8, starting transfers between devices: none -> 9.77 us  [swap(): return lax.ppermute(value, axis, [(i, i ^ k) for i in range(size)])]
    ppermute x0 -> x8, waiting for transfers between devices: none -> 6.1 us  [swap(): return lax.ppermute(value, axis, [(i, i ^ k) for i in range(size)])]
    convert_element_type x1 -> x0, other arithmetic: 1.94 us -> none  [local(): grad_pre = (share * slope).astype(jnp.bfloat16)]
    unnamed x2 -> x6, local copies, waits for them, and re-layouts: 1.1 us -> 1.93 us
  transfers between devices with their start and end apart: 1 -> 8, of which waited for: 1 -> 2; matrix products, arithmetic and copies ran while one was open for 20% -> 0% of each run, Pallas kernels for 0% -> 25%
where the time goes in v1:
time: 57.2 us; the launch traced here: 56.9 us
  Pallas kernels  38.4 us (67%)
  starting transfers between devices  9.77 us (17%)
  waiting for transfers between devices  6.1 us (11%)
  local copies, waits for them, and re-layouts  1.94 us (3%)
  between operations  0.71 us (1%)
    pallas_call x1, Pallas kernels, hidden_grad_call(): pl.pallas_call(functools.partial(hidden_grad_kernel, n, parts, chunks), o...  23.6 us
    pallas_call x1, Pallas kernels, weight_grad_call(): pl.pallas_call(functools.partial(weight_grad_kernel, chunks), out_shape=j...  13.4 us
    ppermute x8, starting transfers between devices, swap(): return lax.ppermute(value, axis, [(i, i ^ k) for i in range(size)])  9.77 us
    ppermute x8, waiting for transfers between devices, swap(): return lax.ppermute(value, axis, [(i, i ^ k) for i in range(size)])  6.1 us
    unnamed x6, local copies, waits for them, and re-layouts  1.93 us
  transfers between devices with their start and end apart: 8, of which 2 were waited for; matrix products, arithmetic and copies ran while one was open for 0% of the time, Pallas kernels for 25%

profile of v1, /device:TPU:0, one launch (start us, length us, event | category | flops | bytes accessed | tf_op | source)
XLA Modules:
  0.0 56.9 jit_solution(11637365350954035319)
XLA Ops:
  0.6 3.1 %collective-permute-start.1 = (bf16[8,3072]{1,0:T(8,128)(2,1)}, bf16[8,3072]{1,0:T(8,128)(2,1)S(1)}, u32[]{:S(2)}, u32[]{:S(2)}) collective-permute-start(bf16[8,3072]{1,0:T(8,128)(2,1)} %refs_0_.1), channel_id=1, source_target_pairs={{0,8},{4,12},{8,0},{12,4},{16,24},{20,28},{24,16},{28,20},{1,9},{5... | collective-permute-start | bytes 147464 | tf_op jit(solution)/shard_map/ppermute | solution.py:218
  3.7 2.6 %collective-permute-start.2 = (bf16[8,3072]{1,0:T(8,128)(2,1)}, bf16[8,3072]{1,0:T(8,128)(2,1)S(1)}, u32[]{:S(2)}, u32[]{:S(2)}) collective-permute-start(bf16[8,3072]{1,0:T(8,128)(2,1)} %refs_0_.1), channel_id=1, source_target_pairs={{0,16},{4,20},{8,24},{12,28},{16,0},{20,4},{24,8},{28,12},{1,17},{... | collective-permute-start | bytes 147464 | tf_op jit(solution)/shard_map/ppermute | solution.py:218
  6.3 0.0 collective-permute-start.3
  6.3 0.0 collective-permute-done.1
  6.3 3.5 %collective-permute-done.2 = bf16[8,3072]{1,0:T(8,128)(2,1)S(1)} collective-permute-done((bf16[8,3072]{1,0:T(8,128)(2,1)}, bf16[8,3072]{1,0:T(8,128)(2,1)S(1)}, u32[]{:S(2)}, u32[]{:S(2)}) %collective-permute-start.2) | collective-permute-done | bytes 49184 | tf_op jit(solution)/shard_map/ppermute | solution.py:218
  9.9 2.5 %collective-permute-done.3 = bf16[8,3072]{1,0:T(8,128)(2,1)S(1)} collective-permute-done((bf16[8,3072]{1,0:T(8,128)(2,1)}, bf16[8,3072]{1,0:T(8,128)(2,1)S(1)}, u32[]{:S(2)}, u32[]{:S(2)}) %collective-permute-start.3) | collective-permute-done | bytes 49184 | tf_op jit(solution)/shard_map/ppermute | solution.py:218
  12.4 0.0 collective-permute-start.4
  12.4 0.5 collective-permute-start
  13.0 0.0 copy-start
  13.0 1.1 %copy-done = bf16[64,6144]{1,0:T(8,128)(2,1)S(1)} copy-done((bf16[64,6144]{1,0:T(8,128)(2,1)S(1)}, bf16[64,6144]{1,0:T(8,128)(2,1)}, u32[]{:S(2)}) %copy-start) | copy-done | bytes 786456
  14.1 0.7 %gelu.1 = (bf16[64,6144]{1,0:T(8,128)(2,1)S(1)}, f32[16,6144]{1,0:T(8,128)S(1)}) custom-call(bf16[64,6144]{1,0:T(8,128)(2,1)S(1)} %copy-done), custom_call_target="tpu_custom_call" | custom-call | flops 7864320 | bytes 1572864 | tf_op jit(solution)/shard_map/gelu/pallas_call | solution.py:82
  14.8 0.0 collective-permute-done.refs_1_
  14.8 0.0 collective-permute-done.4.refs_3_
  14.8 0.0 copy-start.1
  14.8 0.8 %copy-done.1 = bf16[8,3072]{1,0:T(8,128)(2,1)S(1)} copy-done((bf16[8,3072]{1,0:T(8,128)(2,1)S(1)}, bf16[8,3072]{1,0:T(8,128)(2,1)}, u32[]{:S(2)}) %copy-start.1) | copy-done | bytes 49176
  15.6 23.6 %hidden_grad.1 = (bf16[64,3072]{1,0:T(8,128)(2,1)S(1)}, f32[16,6144]{1,0:T(8,128)S(1)}, bf16[16,6144]{1,0:T(8,128)(2,1)S(1)}, bf16[16,6144]{1,0:T(8,128)(2,1)S(1)}, bf16[16,6144]{1,0:T(8,128)(2,1)S(1)}) custom-call(bf16[8,3072]{1,0:T(8,128)(2,1)S(1)} %copy-done.1, bf16[8,3072]{1,0:T(8,128)(2,1)S(1)} %collective-permute-done.refs_1_, ...), custom_call_target="tpu_custom_call" | custom-call | flops 2415919104 | bytes 37748736 | tf_op jit(solution)/shard_map/hidden_grad/pallas_call | solution.py:144
  39.2 1.6 %collective-permute-start.5 = (bf16[16,6144]{1,0:T(8,128)(2,1)S(1)}, bf16[16,6144]{1,0:T(8,128)(2,1)S(1)}, u32[]{:S(2)}, u32[]{:S(2)}) collective-permute-start(bf16[16,6144]{1,0:T(8,128)(2,1)S(1)} %get-tuple-element.11), channel_id=1, source_target_pairs={{0,1},{1,0},{2,3},{3,2},{4,5},{5,4},{6,7},{7,6},{8,9},{9,8},{10,11... | collective-permute-start | bytes 589832 | tf_op jit(solution)/shard_map/ppermute | solution.py:218
  40.8 1.5 %collective-permute-start.6 = (bf16[16,6144]{1,0:T(8,128)(2,1)S(1)}, bf16[16,6144]{1,0:T(8,128)(2,1)S(1)}, u32[]{:S(2)}, u32[]{:S(2)}) collective-permute-start(bf16[16,6144]{1,0:T(8,128)(2,1)S(1)} %get-tuple-element.12), channel_id=1, source_target_pairs={{0,2},{1,3},{2,0},{3,1},{4,6},{5,7},{6,4},{7,5},{8,10},{9,11},{10,... | collective-permute-start | bytes 589832 | tf_op jit(solution)/shard_map/ppermute | solution.py:218
  42.3 0.5 collective-permute-start.7
  42.8 13.4 %weight_grad.1 = bf16[6144,3072]{1,0:T(8,128)(2,1)} custom-call(bf16[64,6144]{1,0:T(8,128)(2,1)S(1)} %get-tuple-element.14.hidden_ref, bf16[64,3072]{1,0:T(8,128)(2,1)S(1)} %get-tuple-element.15.g_ref), custom_call_target="tpu_custom_call" | custom-call | flops 2415919104 | bytes 37748736 | tf_op jit(solution)/shard_map/weight_grad/pallas_call | solution.py:184
  56.1 0.0 collective-permute-done.5.refs_0_
  56.1 0.0 collective-permute-done.6.refs_1_
  56.2 0.0 collective-permute-done.7.refs_2_
  56.2 0.8 %total.1 = bf16[16,6144]{1,0:T(8,128)(2,1)} custom-call(f32[16,6144]{1,0:T(8,128)S(1)} %get-tuple-element.9.own_ref, f32[16,6144]{1,0:T(8,128)S(1)} %get-tuple-element.10.slope_ref, bf16[16,6144]{1,0:T(8,128)(2,1)S(1)} %collective-permute-done.5.refs_0_, bf16[16,6144]{1,0:T(8,128)(2,1)S(1)} %collective-permute-done.6.refs_1_, ...), custom_call_target="tpu_custom_call" | custom-call | tf_op jit(solution)/shard_map/total/pallas_call | solution.py:206
  (3 shorter events, 0.0 us)
Async XLA Ops:
  0.6 5.7 %collective-permute-start.1 = (bf16[8,3072]{1,0:T(8,128)(2,1)}, bf16[8,3072]{1,0:T(8,128)(2,1)S(1)}, u32[]{:S(2)}, u32[]{:S(2)}) collective-permute-start(bf16[8,3072]{1,0:T(8,128)(2,1)} %refs_0_.1), channel_id=1, source_target_pairs={{0,8},{4,12},{8,0},{12,4},{16,24},{20,28},{24,16},{28,20},{1,9},{5... | collective-permute-start | bytes 147464 | tf_op jit(solution)/shard_map/ppermute | solution.py:218
  3.7 6.1 %collective-permute-start.2 = (bf16[8,3072]{1,0:T(8,128)(2,1)}, bf16[8,3072]{1,0:T(8,128)(2,1)S(1)}, u32[]{:S(2)}, u32[]{:S(2)}) collective-permute-start(bf16[8,3072]{1,0:T(8,128)(2,1)} %refs_0_.1), channel_id=1, source_target_pairs={{0,16},{4,20},{8,24},{12,28},{16,0},{20,4},{24,8},{28,12},{1,17},{... | collective-permute-start | bytes 147464 | tf_op jit(solution)/shard_map/ppermute | solution.py:218
  6.3 6.1 %collective-permute-start.3 = (bf16[8,3072]{1,0:T(8,128)(2,1)}, bf16[8,3072]{1,0:T(8,128)(2,1)S(1)}, u32[]{:S(2)}, u32[]{:S(2)}) collective-permute-start(bf16[8,3072]{1,0:T(8,128)(2,1)} %refs_0_.1), channel_id=1, source_target_pairs={{0,24},{4,28},{8,16},{12,20},{16,8},{20,12},{24,0},{28,4},{1,25},{... | collective-permute-start | bytes 147464 | tf_op jit(solution)/shard_map/ppermute | solution.py:218
  12.4 2.4 %collective-permute-start.4 = (bf16[24,3072]{1,0:T(8,128)(2,1)S(1)}, bf16[24,3072]{1,0:T(8,128)(2,1)S(1)}, u32[]{:S(2)}, u32[]{:S(2)}) collective-permute-start(bf16[24,3072]{1,0:T(8,128)(2,1)S(1)} %constant_dynamic-update-slice_fusion.refs_2_), channel_id=1, source_target_pairs={{0,4},{4,0},{8,12},{12,8},{16,20},{20,16},{24,28},{28,24},{1,5},{5... | collective-permute-start | bytes 442376 | tf_op jit(solution)/shard_map/ppermute | solution.py:218
  12.4 2.3 %collective-permute-start = (bf16[8,3072]{1,0:T(8,128)(2,1)}, bf16[8,3072]{1,0:T(8,128)(2,1)S(1)}, u32[]{:S(2)}, u32[]{:S(2)}) collective-permute-start(bf16[8,3072]{1,0:T(8,128)(2,1)} %refs_0_.1), channel_id=1, source_target_pairs={{0,4},{4,0},{8,12},{12,8},{16,20},{20,16},{24,28},{28,24},{1,5},{5... | collective-permute-start | bytes 147464 | tf_op jit(solution)/shard_map/ppermute | solution.py:218
  13.0 1.1 %copy-start = (bf16[64,6144]{1,0:T(8,128)(2,1)S(1)}, bf16[64,6144]{1,0:T(8,128)(2,1)}, u32[]{:S(2)}) copy-start(bf16[64,6144]{1,0:T(8,128)(2,1)} %x_ref.1) | copy-start | bytes 2359300
  14.8 0.8 %copy-start.1 = (bf16[8,3072]{1,0:T(8,128)(2,1)S(1)}, bf16[8,3072]{1,0:T(8,128)(2,1)}, u32[]{:S(2)}) copy-start(bf16[8,3072]{1,0:T(8,128)(2,1)} %refs_0_.1) | copy-start | bytes 147460
  39.2 16.9 %collective-permute-start.5 = (bf16[16,6144]{1,0:T(8,128)(2,1)S(1)}, bf16[16,6144]{1,0:T(8,128)(2,1)S(1)}, u32[]{:S(2)}, u32[]{:S(2)}) collective-permute-start(bf16[16,6144]{1,0:T(8,128)(2,1)S(1)} %get-tuple-element.11), channel_id=1, source_target_pairs={{0,1},{1,0},{2,3},{3,2},{4,5},{5,4},{6,7},{7,6},{8,9},{9,8},{10,11... | collective-permute-start | bytes 589832 | tf_op jit(solution)/shard_map/ppermute | solution.py:218
  40.8 15.4 %collective-permute-start.6 = (bf16[16,6144]{1,0:T(8,128)(2,1)S(1)}, bf16[16,6144]{1,0:T(8,128)(2,1)S(1)}, u32[]{:S(2)}, u32[]{:S(2)}) collective-permute-start(bf16[16,6144]{1,0:T(8,128)(2,1)S(1)} %get-tuple-element.12), channel_id=1, source_target_pairs={{0,2},{1,3},{2,0},{3,1},{4,6},{5,7},{6,4},{7,5},{8,10},{9,11},{10,... | collective-permute-start | bytes 589832 | tf_op jit(solution)/shard_map/ppermute | solution.py:218
  42.3 13.9 %collective-permute-start.7 = (bf16[16,6144]{1,0:T(8,128)(2,1)S(1)}, bf16[16,6144]{1,0:T(8,128)(2,1)S(1)}, u32[]{:S(2)}, u32[]{:S(2)}) collective-permute-start(bf16[16,6144]{1,0:T(8,128)(2,1)S(1)} %get-tuple-element.13), channel_id=1, source_target_pairs={{0,3},{1,2},{2,1},{3,0},{4,7},{5,6},{6,5},{7,4},{8,11},{9,10},{10,... | collective-permute-start | bytes 589832 | tf_op jit(solution)/shard_map/ppermute | solution.py:218

commit v2 on v1

--- a/solution.py
+++ b/solution.py
@@ -51,6 +51,9 @@
 
 
 VMEM = pltpu.VMEM
+CHUNKS = 12
+EARLY = 4
+GROUPS = 2
 
 
 def in_vmem():
@@ -65,7 +68,19 @@
     return pltpu.CompilerParams(vmem_limit_bytes=mib * 1024 * 1024)
 
 
-def gelu_kernel(parts, x_ref, hidden_ref, slope_ref):
+def gelu_kernel(parts, early, x_hbm, g_hbm, w_hbm, hidden_ref, slope_ref, own_ref, w_ref, x_ref, sems):
+    bring_x = pltpu.make_async_copy(x_hbm, x_ref, sems.at[0])
+    bring_g = pltpu.make_async_copy(g_hbm, own_ref, sems.at[1])
+    bring_x.start()
+    bring_g.start()
+    step = w_ref.shape[0] // early
+    bring_w = []
+    for i in range(early):
+        rows = pl.ds(i * step, step)
+        bring_w.append(pltpu.make_async_copy(w_hbm.at[rows], w_ref.at[rows], sems.at[2 + i]))
+    for copy in bring_w:
+        copy.start()
+    bring_x.wait()
     own = lax.axis_index("wid")
     rows = x_ref.shape[0] // parts
     for b in range(parts):
@@ -75,92 +90,130 @@
         hidden_ref[b * rows : (b + 1) * rows, :] = value.astype(BF16)
         if b == 0:
             slope_ref[...] = slope
-
-
-def gelu_call(parts, x):
+    bring_g.wait()
+    for copy in bring_w:
+        copy.wait()
+
+
+def gelu_call(parts, early, x, g, weight):
     tokens, width = x.shape
     return pl.pallas_call(
-        functools.partial(gelu_kernel, parts),
+        functools.partial(gelu_kernel, parts, early),
         out_shape=(
             jax.ShapeDtypeStruct((tokens, width), BF16),
             jax.ShapeDtypeStruct((tokens // parts, width), F32),
-        ),
-        in_specs=[in_vmem()],
-        out_specs=(in_vmem(), in_vmem()),
+            jax.ShapeDtypeStruct(g.shape, BF16),
+            jax.ShapeDtypeStruct((weight.shape[0] * early // CHUNKS, weight.shape[1]), BF16),
+        ),
+        in_specs=[pl.BlockSpec(memory_space=pltpu.HBM)] * 3,
+        out_specs=(in_vmem(),) * 4,
+        scratch_shapes=[VMEM((tokens, width), BF16), pltpu.SemaphoreType.DMA((2 + early,))],
         compiler_params=params(8),
         cost_estimate=pl.CostEstimate(
-            flops=tokens * width * 20, transcendentals=tokens * width, bytes_accessed=4 * tokens * width
+            flops=tokens * width * 20,
+            transcendentals=tokens * width,
+            bytes_accessed=4 * tokens * width + weight.size * 2 * early // CHUNKS,
         ),
         name="gelu",
-    )(x)
-
-
-def hidden_grad_kernel(n, parts, chunks, *refs):
-    own_ref, swap_ref, far_ref, farswap_ref, w_ref = refs[:5]
-    g_out, own_out = refs[5:7]
-    sends = refs[7 : 7 + parts - 1]
-    w_buf, g_buf, sems = refs[7 + parts - 1 :]
-    chunk = w_ref.shape[0] // chunks
-    copies = [
-        pltpu.make_async_copy(
-            w_ref.at[pl.ds(i * chunk, chunk)], w_buf.at[pl.ds(i * chunk, chunk)], sems.at[i]
-        )
-        for i in range(chunks)
-    ]
-    for copy in copies:
-        copy.start()
+    )(x, g, weight)
+
+
+def join_kernel(*refs):
+    rows = refs[0].shape[0]
+    for j, ref in enumerate(refs[:-1]):
+        refs[-1][j * rows : (j + 1) * rows, :] = ref[...]
+
+
+def join_call(blocks):
+    rows, width = blocks[0].shape
+    return pl.pallas_call(
+        join_kernel,
+        out_shape=jax.ShapeDtypeStruct((len(blocks) * rows, width), BF16),
+        in_specs=[in_vmem()] * len(blocks),
+        out_specs=in_vmem(),
+        compiler_params=params(2),
+        name="join",
+    )(*blocks)
+
+
+def hidden_grad_kernel(n, parts, early, groups, *refs):
+    near_ref, swap_ref, w_hbm, held_ref = refs[:4]
+    g_out, own_out = refs[4:6]
+    sends = refs[6 : 6 + parts - 1]
+    w_ref, g_buf, sems = refs[6 + parts - 1 :]
+    late = CHUNKS - early
+    step = w_ref.shape[0] // late
+
+    def bring(i):
+        source = w_hbm.at[pl.ds(pl.multiple_of((early + i) * step, step), step)]
+        return pltpu.make_async_copy(source, w_ref.at[pl.ds(pl.multiple_of(i * step, step), step)], sems.at[i])
+
+    for i in range(late):
+        bring(i).start()
     hid = lax.axis_index("hid")
     wid = lax.axis_index("wid")
-    rows = own_ref.shape[0]
+    rows = near_ref.shape[0] // (n // 2)
     per = n // parts
 
-    def place(source):
+    def place(k):
+        source = lax.bitwise_xor(hid, k)
         block = lax.bitwise_xor(source // per, wid)
         return block * per + lax.rem(source, per)
 
-    g_buf[place(hid)] = own_ref[...]
-    g_buf[place(lax.bitwise_xor(hid, 1))] = swap_ref[...]
-    for j in range(n // 2 - 1):
-        k = 2 * (j + 1)
-        g_buf[place(lax.bitwise_xor(hid, k))] = far_ref[j * rows : (j + 1) * rows]
-        g_buf[place(lax.bitwise_xor(hid, k ^ 1))] = farswap_ref[j * rows : (j + 1) * rows]
-    g = g_buf[...].reshape(n * rows, own_ref.shape[1])
-    g_out[...] = g
+    for j in range(n // 2):
+        g_buf[place(2 * j)] = near_ref[j * rows : (j + 1) * rows]
+        g_buf[place(2 * j + 1)] = swap_ref[j * rows : (j + 1) * rows]
+    g_out[...] = g_buf[...].reshape(g_out.shape)
     share = n * rows // parts
-    for i, copy in enumerate(copies):
-        copy.wait()
-        part = contract_cols(w_buf[i * chunk : (i + 1) * chunk], g).T
-        columns = slice(i * chunk, (i + 1) * chunk)
-        own_out[:, columns] = part[:share]
+
+    def multiply(w, at):
+        part = contract_cols(w, g_out[...]).T
+        own_out[:, pl.ds(at, step)] = part[:share]
         for k in range(1, parts):
-            sends[k - 1][:, columns] = part[k * share : (k + 1) * share].astype(BF16)
-
-
-def hidden_grad_call(n, parts, chunks, own, swap, far, farswap, weight):
-    rows, width = own.shape
+            sends[k - 1][:, pl.ds(at, step)] = part[k * share : (k + 1) * share].astype(BF16)
+
+    for j in range(early):
+        multiply(held_ref[j * step : (j + 1) * step], j * step)
+    each = late // groups
+
+    def group(i, unused):
+        for j in range(each):
+            bring(i * each + j).wait()
+        for j in range(each):
+            at = pl.multiple_of((i * each + j) * step, step)
+            multiply(w_ref[pl.ds(at, step)], pl.multiple_of(at + early * step, step))
+        return unused
+
+    lax.fori_loop(0, groups, group, 0)
+
+
+def hidden_grad_call(n, parts, early, groups, near, swap, weight, held):
+    width = near.shape[1]
+    tokens = 2 * near.shape[0]
     ff = weight.shape[0]
-    tokens = n * rows
     share = tokens // parts
-    return pl.pallas_call(
-        functools.partial(hidden_grad_kernel, n, parts, chunks),
+    late = CHUNKS - early
+    outs = pl.pallas_call(
+        functools.partial(hidden_grad_kernel, n, parts, early, groups),
         out_shape=(
             jax.ShapeDtypeStruct((tokens, width), BF16),
             jax.ShapeDtypeStruct((share, ff), F32),
             *[jax.ShapeDtypeStruct((share, ff), BF16)] * (parts - 1),
         ),
-        in_specs=[in_vmem()] * 4 + [anywhere()],
+        in_specs=[in_vmem()] * 2 + [anywhere(), in_vmem()],
         out_specs=tuple([in_vmem()] * (parts + 1)),
         scratch_shapes=[
-            VMEM((ff, width), BF16),
-            VMEM((n, rows, width), BF16),
-            pltpu.SemaphoreType.DMA((chunks,)),
+            VMEM((ff * late // CHUNKS, width), BF16),
+            VMEM((n, tokens // n, width), BF16),
+            pltpu.SemaphoreType.DMA((late,)),
         ],
-        compiler_params=params(48),
+        compiler_params=params(32),
         cost_estimate=pl.CostEstimate(
             flops=2 * tokens * width * ff, transcendentals=0, bytes_accessed=2 * width * ff
         ),
         name="hidden_grad",
-    )(own, swap, far, farswap, weight)
+    )(near, swap, weight, held)
+    return outs[0], outs[1], outs[2:]
 
 
 def weight_grad_kernel(chunks, hidden_ref, g_ref, out_ref, buf, sems):
@@ -213,18 +266,17 @@
     )(own, slope, *received)
 
 
-def ring(n, parts, chunks, grad_out, pre_act, weight):
+def ring(n, parts, grad_out, pre_act, weight):
     def swap(value, axis, size, k):
         return lax.ppermute(value, axis, [(i, i ^ k) for i in range(size)])
 
-    own_swap = swap(grad_out, "hid", n, 1)
     far = [swap(grad_out, "hid", n, k) for k in range(2, n, 2)]
-    hidden, slope = gelu_call(parts, pre_act)
-    far = jnp.concatenate(far, axis=0)
-    far_swap = swap(far, "hid", n, 1)
-    g, own, *sends = hidden_grad_call(n, parts, chunks, grad_out, own_swap, far, far_swap, weight)
+    hidden, slope, own_rows, held = gelu_call(parts, EARLY, pre_act, grad_out, weight)
+    near = join_call([own_rows, *far])
+    other = swap(near, "hid", n, 1)
+    g, own, sends = hidden_grad_call(n, parts, EARLY, GROUPS, near, other, weight, held)
     received = [swap(s, "wid", parts, k + 1) for k, s in enumerate(sends)]
-    grad_w = weight_grad_call(chunks, hidden, g)
+    grad_w = weight_grad_call(CHUNKS, hidden, g)
     return (sum_call(own, slope, received), grad_w)
 
 
@@ -237,10 +289,9 @@
 
     def local(grad_out, pre_act, weight):
         ff, width = weight.shape
-        chunk = 512
         small = power_of_two(n) and power_of_two(parts) and parts < n <= 8
-        if small and ff % chunk == 0 and width % 256 == 0 and ff * width * 2 <= 40 * 2**20:
-            return ring(n, parts, ff // chunk, grad_out, pre_act, weight)
+        if small and ff % (CHUNKS * 256) == 0 and width % 256 == 0 and ff * width * 2 <= 40 * 2**20:
+            return ring(n, parts, grad_out, pre_act, weight)
         return plain(grad_out, pre_act, weight)
 
     return jax.shard_map(

time: 57.2 us -> 44.6 us (0.78)
  Pallas kernels: 38.4 us -> 31 us
  waiting for transfers between devices: 6.1 us -> 1.44 us
    pallas_call x2 -> x3, Pallas kernels: 24.3 us -> 16.8 us  [the longest x1 12 us: hidden_grad_call(): pl.pallas_call(functools.partial(hidden_grad_kernel, n, parts, early, gro...]
    ppermute x8 -> x7, waiting for transfers between devices: 6.1 us -> 1.44 us  [swap(): return lax.ppermute(value, axis, [(i, i ^ k) for i in range(size)])]
    ppermute x8 -> x7, starting transfers between devices: 9.77 us -> 9.33 us  [swap(): return lax.ppermute(value, axis, [(i, i ^ k) for i in range(size)])]
    unnamed x6 -> x4, local copies, waits for them, and re-layouts: 1.93 us -> 1.93 us
  transfers between devices with their start and end apart: 8 -> 7, of which waited for: 2 -> 1; matrix products, arithmetic and copies ran while one was open for 0% -> 0% of each run, Pallas kernels for 25% -> 41%
where the time goes in v2:
time: 44.6 us; the launch traced here: 44.4 us
  Pallas kernels  31 us (70%)
  starting transfers between devices  9.33 us (21%)
  local copies, waits for them, and re-layouts  1.93 us (4%)
  waiting for transfers between devices  1.44 us (3%)
  between operations  0.72 us (2%)
    pallas_call x1, Pallas kernels, weight_grad_call(): pl.pallas_call(functools.partial(weight_grad_kernel, chunks), out_shape=j...  13.4 us
    pallas_call x1, Pallas kernels, hidden_grad_call(): pl.pallas_call(functools.partial(hidden_grad_kernel, n, parts, early, gro...  12 us
    ppermute x7, starting transfers between devices, swap(): return lax.ppermute(value, axis, [(i, i ^ k) for i in range(size)])  9.33 us
    pallas_call x1, Pallas kernels, gelu_call(): pl.pallas_call(functools.partial(gelu_kernel, parts, early), out_shape=(j...  4.81 us
    unnamed x4, local copies, waits for them, and re-layouts  1.93 us
    ppermute x7, waiting for transfers between devices, swap(): return lax.ppermute(value, axis, [(i, i ^ k) for i in range(size)])  1.44 us
  transfers between devices with their start and end apart: 7, of which 1 were waited for; matrix products, arithmetic and copies ran while one was open for 0% of the time, Pallas kernels for 41%

profile of v2, /device:TPU:0, one launch (start us, length us, event | category | flops | bytes accessed | tf_op | source)
XLA Modules:
  0.0 44.4 jit_solution(18062503530866727612)
XLA Ops:
  0.6 3.1 %collective-permute-start = (bf16[8,3072]{1,0:T(8,128)(2,1)}, bf16[8,3072]{1,0:T(8,128)(2,1)S(1)}, u32[]{:S(2)}, u32[]{:S(2)}) collective-permute-start(bf16[8,3072]{1,0:T(8,128)(2,1)} %g_hbm.1), channel_id=1, source_target_pairs={{0,8},{4,12},{8,0},{12,4},{16,24},{20,28},{24,16},{28,20},{1,9},{5... | collective-permute-start | bytes 147464 | tf_op jit(solution)/shard_map/ppermute | solution.py:271
  3.7 2.5 %collective-permute-start.2 = (bf16[8,3072]{1,0:T(8,128)(2,1)}, bf16[8,3072]{1,0:T(8,128)(2,1)S(1)}, u32[]{:S(2)}, u32[]{:S(2)}) collective-permute-start(bf16[8,3072]{1,0:T(8,128)(2,1)} %g_hbm.1), channel_id=1, source_target_pairs={{0,24},{4,28},{8,16},{12,20},{16,8},{20,12},{24,0},{28,4},{1,25},{... | collective-permute-start | bytes 147464 | tf_op jit(solution)/shard_map/ppermute | solution.py:271
  6.2 0.1 collective-permute-start.1
  6.3 0.0 copy-start
  6.3 1.1 %copy-done = bf16[64,6144]{1,0:T(8,128)(2,1)S(1)} copy-done((bf16[64,6144]{1,0:T(8,128)(2,1)S(1)}, bf16[64,6144]{1,0:T(8,128)(2,1)}, u32[]{:S(2)}) %copy-start) | copy-done | bytes 786456
  7.5 0.0 copy-start.1
  7.5 0.8 %copy-done.1 = bf16[8,3072]{1,0:T(8,128)(2,1)S(1)} copy-done((bf16[8,3072]{1,0:T(8,128)(2,1)S(1)}, bf16[8,3072]{1,0:T(8,128)(2,1)}, u32[]{:S(2)}) %copy-start.1) | copy-done | bytes 49176
  8.3 4.8 %gelu.1 = (bf16[64,6144]{1,0:T(8,128)(2,1)S(1)}, f32[16,6144]{1,0:T(8,128)S(1)}, bf16[8,3072]{1,0:T(8,128)(2,1)S(1)}, bf16[2048,3072]{1,0:T(8,128)(2,1)S(1)}) custom-call(bf16[64,6144]{1,0:T(8,128)(2,1)S(1)} %copy-done, bf16[8,3072]{1,0:T(8,128)(2,1)S(1)} %copy-done.1, bf16[6144,3072]{1,0:T(8,128)(2,1)} %refs_2_.1), custom_call_target="tpu_custom_call" | custom-call | flops 7864320 | bytes 14155776 | tf_op jit(solution)/shard_map/gelu/pallas_call | solution.py:100
  13.1 0.0 collective-permute-done.refs_1_
  13.1 0.0 collective-permute-done.2.refs_3_
  13.1 0.0 collective-permute-done.1.refs_2_
  13.1 0.1 collective-permute-start.3
  13.2 1.4 %collective-permute-done.3.refs_1_ = bf16[32,3072]{1,0:T(8,128)(2,1)S(1)} collective-permute-done((bf16[32,3072]{1,0:T(8,128)(2,1)S(1)}, bf16[32,3072]{1,0:T(8,128)(2,1)S(1)}, u32[]{:S(2)}, u32[]{:S(2)}) %collective-permute-start.3) | collective-permute-done | bytes 196640 | tf_op jit(solution)/shard_map/ppermute | solution.py:271
  14.7 12.0 %hidden_grad.1 = (bf16[64,3072]{1,0:T(8,128)(2,1)S(1)}, f32[16,6144]{1,0:T(8,128)S(1)}, bf16[16,6144]{1,0:T(8,128)(2,1)S(1)}, bf16[16,6144]{1,0:T(8,128)(2,1)S(1)}, bf16[16,6144]{1,0:T(8,128)(2,1)S(1)}) custom-call(bf16[32,3072]{1,0:T(8,128)(2,1)S(1)} %join.1.refs_0_, bf16[32,3072]{1,0:T(8,128)(2,1)S(1)} %collective-permute-done.3.refs_1_, ...), custom_call_target="tpu_custom_call" | custom-call | flops 2415919104 | bytes 37748736 | tf_op jit(solution)/shard_map/hidden_grad/pallas_call | solution.py:196
  26.7 1.6 %collective-permute-start.4 = (bf16[16,6144]{1,0:T(8,128)(2,1)S(1)}, bf16[16,6144]{1,0:T(8,128)(2,1)S(1)}, u32[]{:S(2)}, u32[]{:S(2)}) collective-permute-start(bf16[16,6144]{1,0:T(8,128)(2,1)S(1)} %get-tuple-element.15), channel_id=1, source_target_pairs={{0,1},{1,0},{2,3},{3,2},{4,5},{5,4},{6,7},{7,6},{8,9},{9,8},{10,11... | collective-permute-start | bytes 589832 | tf_op jit(solution)/shard_map/ppermute | solution.py:271
  28.2 1.5 %collective-permute-start.5 = (bf16[16,6144]{1,0:T(8,128)(2,1)S(1)}, bf16[16,6144]{1,0:T(8,128)(2,1)S(1)}, u32[]{:S(2)}, u32[]{:S(2)}) collective-permute-start(bf16[16,6144]{1,0:T(8,128)(2,1)S(1)} %get-tuple-element.16), channel_id=1, source_target_pairs={{0,2},{1,3},{2,0},{3,1},{4,6},{5,7},{6,4},{7,5},{8,10},{9,11},{10,... | collective-permute-start | bytes 589832 | tf_op jit(solution)/shard_map/ppermute | solution.py:271
  29.7 0.5 %collective-permute-start.6 = (bf16[16,6144]{1,0:T(8,128)(2,1)S(1)}, bf16[16,6144]{1,0:T(8,128)(2,1)S(1)}, u32[]{:S(2)}, u32[]{:S(2)}) collective-permute-start(bf16[16,6144]{1,0:T(8,128)(2,1)S(1)} %get-tuple-element.17), channel_id=1, source_target_pairs={{0,3},{1,2},{2,1},{3,0},{4,7},{5,6},{6,5},{7,4},{8,11},{9,10},{10,... | collective-permute-start | bytes 589832 | tf_op jit(solution)/shard_map/ppermute | solution.py:271
  30.2 13.4 %weight_grad.1 = bf16[6144,3072]{1,0:T(8,128)(2,1)} custom-call(bf16[64,6144]{1,0:T(8,128)(2,1)S(1)} %get-tuple-element.18.hidden_ref, bf16[64,3072]{1,0:T(8,128)(2,1)S(1)} %get-tuple-element.19.g_ref), custom_call_target="tpu_custom_call" | custom-call | flops 2415919104 | bytes 37748736 | tf_op jit(solution)/shard_map/weight_grad/pallas_call | solution.py:237
  43.6 0.0 collective-permute-done.4.refs_0_
  43.6 0.0 collective-permute-done.5.refs_1_
  43.6 0.0 collective-permute-done.6.refs_2_
  43.6 0.8 %total.1 = bf16[16,6144]{1,0:T(8,128)(2,1)} custom-call(f32[16,6144]{1,0:T(8,128)S(1)} %get-tuple-element.13.own_ref, f32[16,6144]{1,0:T(8,128)S(1)} %get-tuple-element.14.slope_ref, bf16[16,6144]{1,0:T(8,128)(2,1)S(1)} %collective-permute-done.4.refs_0_, bf16[16,6144]{1,0:T(8,128)(2,1)S(1)} %collective-permute-done.5.refs_1_, ...), custom_call_target="tpu_custom_call" | custom-call | tf_op jit(solution)/shard_map/total/pallas_call | solution.py:259
  (1 shorter events, 0.0 us)
Async XLA Ops:
  0.6 12.5 %collective-permute-start = (bf16[8,3072]{1,0:T(8,128)(2,1)}, bf16[8,3072]{1,0:T(8,128)(2,1)S(1)}, u32[]{:S(2)}, u32[]{:S(2)}) collective-permute-start(bf16[8,3072]{1,0:T(8,128)(2,1)} %g_hbm.1), channel_id=1, source_target_pairs={{0,8},{4,12},{8,0},{12,4},{16,24},{20,28},{24,16},{28,20},{1,9},{5... | collective-permute-start | bytes 147464 | tf_op jit(solution)/shard_map/ppermute | solution.py:271
  3.7 9.4 %collective-permute-start.2 = (bf16[8,3072]{1,0:T(8,128)(2,1)}, bf16[8,3072]{1,0:T(8,128)(2,1)S(1)}, u32[]{:S(2)}, u32[]{:S(2)}) collective-permute-start(bf16[8,3072]{1,0:T(8,128)(2,1)} %g_hbm.1), channel_id=1, source_target_pairs={{0,24},{4,28},{8,16},{12,20},{16,8},{20,12},{24,0},{28,4},{1,25},{... | collective-permute-start | bytes 147464 | tf_op jit(solution)/shard_map/ppermute | solution.py:271
  6.2 6.9 %collective-permute-start.1 = (bf16[8,3072]{1,0:T(8,128)(2,1)}, bf16[8,3072]{1,0:T(8,128)(2,1)S(1)}, u32[]{:S(2)}, u32[]{:S(2)}) collective-permute-start(bf16[8,3072]{1,0:T(8,128)(2,1)} %g_hbm.1), channel_id=1, source_target_pairs={{0,16},{4,20},{8,24},{12,28},{16,0},{20,4},{24,8},{28,12},{1,17},{... | collective-permute-start | bytes 147464 | tf_op jit(solution)/shard_map/ppermute | solution.py:271
  6.3 1.1 %copy-start = (bf16[64,6144]{1,0:T(8,128)(2,1)S(1)}, bf16[64,6144]{1,0:T(8,128)(2,1)}, u32[]{:S(2)}) copy-start(bf16[64,6144]{1,0:T(8,128)(2,1)} %x_hbm.1) | copy-start | bytes 2359300
  7.5 0.8 %copy-start.1 = (bf16[8,3072]{1,0:T(8,128)(2,1)S(1)}, bf16[8,3072]{1,0:T(8,128)(2,1)}, u32[]{:S(2)}) copy-start(bf16[8,3072]{1,0:T(8,128)(2,1)} %g_hbm.1) | copy-start | bytes 147460
  13.1 1.5 %collective-permute-start.3 = (bf16[32,3072]{1,0:T(8,128)(2,1)S(1)}, bf16[32,3072]{1,0:T(8,128)(2,1)S(1)}, u32[]{:S(2)}, u32[]{:S(2)}) collective-permute-start(bf16[32,3072]{1,0:T(8,128)(2,1)S(1)} %join.1.refs_0_), channel_id=1, source_target_pairs={{0,4},{4,0},{8,12},{12,8},{16,20},{20,16},{24,28},{28,24},{1,5},{5... | collective-permute-start | bytes 589832 | tf_op jit(solution)/shard_map/ppermute | solution.py:271
  26.7 16.9 %collective-permute-start.4 = (bf16[16,6144]{1,0:T(8,128)(2,1)S(1)}, bf16[16,6144]{1,0:T(8,128)(2,1)S(1)}, u32[]{:S(2)}, u32[]{:S(2)}) collective-permute-start(bf16[16,6144]{1,0:T(8,128)(2,1)S(1)} %get-tuple-element.15), channel_id=1, source_target_pairs={{0,1},{1,0},{2,3},{3,2},{4,5},{5,4},{6,7},{7,6},{8,9},{9,8},{10,11... | collective-permute-start | bytes 589832 | tf_op jit(solution)/shard_map/ppermute | solution.py:271
  28.2 15.4 %collective-permute-start.5 = (bf16[16,6144]{1,0:T(8,128)(2,1)S(1)}, bf16[16,6144]{1,0:T(8,128)(2,1)S(1)}, u32[]{:S(2)}, u32[]{:S(2)}) collective-permute-start(bf16[16,6144]{1,0:T(8,128)(2,1)S(1)} %get-tuple-element.16), channel_id=1, source_target_pairs={{0,2},{1,3},{2,0},{3,1},{4,6},{5,7},{6,4},{7,5},{8,10},{9,11},{10,... | collective-permute-start | bytes 589832 | tf_op jit(solution)/shard_map/ppermute | solution.py:271
  29.7 13.9 %collective-permute-start.6 = (bf16[16,6144]{1,0:T(8,128)(2,1)S(1)}, bf16[16,6144]{1,0:T(8,128)(2,1)S(1)}, u32[]{:S(2)}, u32[]{:S(2)}) collective-permute-start(bf16[16,6144]{1,0:T(8,128)(2,1)S(1)} %get-tuple-element.17), channel_id=1, source_target_pairs={{0,3},{1,2},{2,1},{3,0},{4,7},{5,6},{6,5},{7,4},{8,11},{9,10},{10,... | collective-permute-start | bytes 589832 | tf_op jit(solution)/shard_map/ppermute | solution.py:271

commit v3 on v2

--- a/solution.py
+++ b/solution.py
@@ -52,8 +52,8 @@
 
 VMEM = pltpu.VMEM
 CHUNKS = 12
-EARLY = 4
-GROUPS = 2
+EARLY = 3
+GROUPS = 3
 
 
 def in_vmem():
@@ -115,7 +115,7 @@
             bytes_accessed=4 * tokens * width + weight.size * 2 * early // CHUNKS,
         ),
         name="gelu",
-    )(x, g, weight)
+    )(*[pltpu.with_memory_space_constraint(v, pltpu.HBM) for v in (x, g, weight)])
 
 
 def join_kernel(*refs):
@@ -216,30 +216,31 @@
     return outs[0], outs[1], outs[2:]
 
 
-def weight_grad_kernel(chunks, hidden_ref, g_ref, out_ref, buf, sems):
-    chunk = out_ref.shape[0] // chunks
+def weight_grad_kernel(sizes, hidden_ref, g_ref, out_ref, buf, sems):
     copies = []
-    for i in range(chunks):
-        rows = pl.ds(i * chunk, chunk)
-        buf[i * chunk : (i + 1) * chunk] = contract_rows(
-            hidden_ref[:, i * chunk : (i + 1) * chunk], g_ref[...]
-        ).astype(BF16)
+    at = 0
+    for i, size in enumerate(sizes):
+        rows = pl.ds(at, size)
+        buf[rows] = contract_rows(hidden_ref[:, rows], g_ref[...]).astype(BF16)
         copy = pltpu.make_async_copy(buf.at[rows], out_ref.at[rows], sems.at[i])
         copy.start()
         copies.append(copy)
+        at += size
     for copy in copies:
         copy.wait()
 
 
-def weight_grad_call(chunks, hidden, g):
+def weight_grad_call(hidden, g):
     tokens, ff = hidden.shape
     width = g.shape[1]
+    step = ff // CHUNKS
+    sizes = [step // 2] * (2 * CHUNKS)
     return pl.pallas_call(
-        functools.partial(weight_grad_kernel, chunks),
+        functools.partial(weight_grad_kernel, sizes),
         out_shape=jax.ShapeDtypeStruct((ff, width), BF16),
         in_specs=[in_vmem()] * 2,
         out_specs=anywhere(),
-        scratch_shapes=[VMEM((ff, width), BF16), pltpu.SemaphoreType.DMA((chunks,))],
+        scratch_shapes=[VMEM((ff, width), BF16), pltpu.SemaphoreType.DMA((len(sizes),))],
         compiler_params=params(48),
         cost_estimate=pl.CostEstimate(
             flops=2 * tokens * width * ff, transcendentals=0, bytes_accessed=2 * width * ff
@@ -270,13 +271,13 @@
     def swap(value, axis, size, k):
         return lax.ppermute(value, axis, [(i, i ^ k) for i in range(size)])
 
-    far = [swap(grad_out, "hid", n, k) for k in range(2, n, 2)]
+    far = [swap(grad_out, "hid", n, k) for k in range(n - 2, 0, -2)][::-1]
     hidden, slope, own_rows, held = gelu_call(parts, EARLY, pre_act, grad_out, weight)
     near = join_call([own_rows, *far])
     other = swap(near, "hid", n, 1)
     g, own, sends = hidden_grad_call(n, parts, EARLY, GROUPS, near, other, weight, held)
     received = [swap(s, "wid", parts, k + 1) for k, s in enumerate(sends)]
-    grad_w = weight_grad_call(CHUNKS, hidden, g)
+    grad_w = weight_grad_call(hidden, g)
     return (sum_call(own, slope, received), grad_w)
 
 

time: 44.6 us -> 43.1 us (0.966)
  local copies, waits for them, and re-layouts: 1.93 us -> 0 us
  waiting for transfers between devices: 1.44 us -> 2.98 us
  Pallas kernels: 31 us -> 29.9 us
    unnamed x4 -> x0, local copies, waits for them, and re-layouts: 1.93 us -> none
    ppermute x7, waiting for transfers between devices: 1.44 us -> 2.98 us  [swap(): return lax.ppermute(value, axis, [(i, i ^ k) for i in range(size)])]
    pallas_call x1, Pallas kernels: 4.81 us -> 4.05 us  [gelu_call(): pl.pallas_call(functools.partial(gelu_kernel, parts, early), out_shape=(j...]
  transfers between devices with their start and end apart: 7 -> 7, of which waited for: 1 -> 3; matrix products, arithmetic and copies ran while one was open for 0% -> 0% of each run, Pallas kernels for 41% -> 40%
where the time goes in v3:
time: 43.1 us; the launch traced here: 43 us
  Pallas kernels  29.9 us (69%)
  starting transfers between devices  9.33 us (22%)
  waiting for transfers between devices  2.98 us (7%)
  between operations  0.7 us (2%)
    pallas_call x1, Pallas kernels, weight_grad_call(): pl.pallas_call(functools.partial(weight_grad_kernel, sizes), out_shape=ja...  13 us
    pallas_call x1, Pallas kernels, hidden_grad_call(): pl.pallas_call(functools.partial(hidden_grad_kernel, n, parts, early, gro...  12.1 us
    ppermute x7, starting transfers between devices, swap(): return lax.ppermute(value, axis, [(i, i ^ k) for i in range(size)])  9.33 us
    pallas_call x1, Pallas kernels, gelu_call(): pl.pallas_call(functools.partial(gelu_kernel, parts, early), out_shape=(j...  4.05 us
    ppermute x7, waiting for transfers between devices, swap(): return lax.ppermute(value, axis, [(i, i ^ k) for i in range(size)])  2.98 us
  transfers between devices with their start and end apart: 7, of which 3 were waited for; matrix products, arithmetic and copies ran while one was open for 0% of the time, Pallas kernels for 40%

profile of v3, /device:TPU:0, one launch (start us, length us, event | category | flops | bytes accessed | tf_op | source)
XLA Modules:
  0.0 43.0 jit_solution(9179834983852260289)
XLA Ops:
  0.6 3.1 %collective-permute-start = (bf16[8,3072]{1,0:T(8,128)(2,1)}, bf16[8,3072]{1,0:T(8,128)(2,1)S(1)}, u32[]{:S(2)}, u32[]{:S(2)}) collective-permute-start(bf16[8,3072]{1,0:T(8,128)(2,1)} %g_hbm.1), channel_id=1, source_target_pairs={{0,8},{4,12},{8,0},{12,4},{16,24},{20,28},{24,16},{28,20},{1,9},{5... | collective-permute-start | bytes 147464 | tf_op jit(solution)/shard_map/ppermute | solution.py:272
  3.7 2.5 %collective-permute-start.2 = (bf16[8,3072]{1,0:T(8,128)(2,1)}, bf16[8,3072]{1,0:T(8,128)(2,1)S(1)}, u32[]{:S(2)}, u32[]{:S(2)}) collective-permute-start(bf16[8,3072]{1,0:T(8,128)(2,1)} %g_hbm.1), channel_id=1, source_target_pairs={{0,24},{4,28},{8,16},{12,20},{16,8},{20,12},{24,0},{28,4},{1,25},{... | collective-permute-start | bytes 147464 | tf_op jit(solution)/shard_map/ppermute | solution.py:272
  6.2 0.1 collective-permute-start.1
  6.3 4.0 %gelu.1 = (bf16[64,6144]{1,0:T(8,128)(2,1)S(1)}, f32[16,6144]{1,0:T(8,128)S(1)}, bf16[8,3072]{1,0:T(8,128)(2,1)S(1)}, bf16[1536,3072]{1,0:T(8,128)(2,1)S(1)}) custom-call(bf16[64,6144]{1,0:T(8,128)(2,1)} %x_hbm.1, bf16[8,3072]{1,0:T(8,128)(2,1)} %g_hbm.1, bf16[6144,3072]{1,0:T(8,128)(2,1)} %refs_2_.1), custom_call_target="tpu_custom_call" | custom-call | flops 7864320 | bytes 11010048 | tf_op jit(solution)/shard_map/gelu/pallas_call | solution.py:100
  10.4 0.0 collective-permute-done.refs_1_
  10.4 0.1 collective-permute-done.2.refs_3_
  10.5 1.5 %collective-permute-done.1.refs_2_ = bf16[8,3072]{1,0:T(8,128)(2,1)S(1)} collective-permute-done((bf16[8,3072]{1,0:T(8,128)(2,1)}, bf16[8,3072]{1,0:T(8,128)(2,1)S(1)}, u32[]{:S(2)}, u32[]{:S(2)}) %collective-permute-start.1) | collective-permute-done | bytes 49184 | tf_op jit(solution)/shard_map/ppermute | solution.py:272
  12.0 0.1 collective-permute-start.3
  12.0 1.4 %collective-permute-done.3.refs_1_ = bf16[32,3072]{1,0:T(8,128)(2,1)S(1)} collective-permute-done((bf16[32,3072]{1,0:T(8,128)(2,1)S(1)}, bf16[32,3072]{1,0:T(8,128)(2,1)S(1)}, u32[]{:S(2)}, u32[]{:S(2)}) %collective-permute-start.3) | collective-permute-done | bytes 196640 | tf_op jit(solution)/shard_map/ppermute | solution.py:272
  13.5 12.1 %hidden_grad.1 = (bf16[64,3072]{1,0:T(8,128)(2,1)S(1)}, f32[16,6144]{1,0:T(8,128)S(1)}, bf16[16,6144]{1,0:T(8,128)(2,1)S(1)}, bf16[16,6144]{1,0:T(8,128)(2,1)S(1)}, bf16[16,6144]{1,0:T(8,128)(2,1)S(1)}) custom-call(bf16[32,3072]{1,0:T(8,128)(2,1)S(1)} %join.1.refs_0_, bf16[32,3072]{1,0:T(8,128)(2,1)S(1)} %collective-permute-done.3.refs_1_, ...), custom_call_target="tpu_custom_call" | custom-call | flops 2415919104 | bytes 37748736 | tf_op jit(solution)/shard_map/hidden_grad/pallas_call | solution.py:196
  25.6 1.6 %collective-permute-start.4 = (bf16[16,6144]{1,0:T(8,128)(2,1)S(1)}, bf16[16,6144]{1,0:T(8,128)(2,1)S(1)}, u32[]{:S(2)}, u32[]{:S(2)}) collective-permute-start(bf16[16,6144]{1,0:T(8,128)(2,1)S(1)} %get-tuple-element.15), channel_id=1, source_target_pairs={{0,1},{1,0},{2,3},{3,2},{4,5},{5,4},{6,7},{7,6},{8,9},{9,8},{10,11... | collective-permute-start | bytes 589832 | tf_op jit(solution)/shard_map/ppermute | solution.py:272
  27.2 1.5 %collective-permute-start.5 = (bf16[16,6144]{1,0:T(8,128)(2,1)S(1)}, bf16[16,6144]{1,0:T(8,128)(2,1)S(1)}, u32[]{:S(2)}, u32[]{:S(2)}) collective-permute-start(bf16[16,6144]{1,0:T(8,128)(2,1)S(1)} %get-tuple-element.16), channel_id=1, source_target_pairs={{0,2},{1,3},{2,0},{3,1},{4,6},{5,7},{6,4},{7,5},{8,10},{9,11},{10,... | collective-permute-start | bytes 589832 | tf_op jit(solution)/shard_map/ppermute | solution.py:272
  28.7 0.5 %collective-permute-start.6 = (bf16[16,6144]{1,0:T(8,128)(2,1)S(1)}, bf16[16,6144]{1,0:T(8,128)(2,1)S(1)}, u32[]{:S(2)}, u32[]{:S(2)}) collective-permute-start(bf16[16,6144]{1,0:T(8,128)(2,1)S(1)} %get-tuple-element.17), channel_id=1, source_target_pairs={{0,3},{1,2},{2,1},{3,0},{4,7},{5,6},{6,5},{7,4},{8,11},{9,10},{10,... | collective-permute-start | bytes 589832 | tf_op jit(solution)/shard_map/ppermute | solution.py:272
  29.2 13.0 %weight_grad.1 = bf16[6144,3072]{1,0:T(8,128)(2,1)} custom-call(bf16[64,6144]{1,0:T(8,128)(2,1)S(1)} %get-tuple-element.18.hidden_ref, bf16[64,3072]{1,0:T(8,128)(2,1)S(1)} %get-tuple-element.19.g_ref), custom_call_target="tpu_custom_call" | custom-call | flops 2415919104 | bytes 37748736 | tf_op jit(solution)/shard_map/weight_grad/pallas_call | solution.py:238
  42.2 0.0 collective-permute-done.4.refs_0_
  42.2 0.0 collective-permute-done.5.refs_1_
  42.2 0.0 collective-permute-done.6.refs_2_
  42.2 0.8 %total.1 = bf16[16,6144]{1,0:T(8,128)(2,1)} custom-call(f32[16,6144]{1,0:T(8,128)S(1)} %get-tuple-element.13.own_ref, f32[16,6144]{1,0:T(8,128)S(1)} %get-tuple-element.14.slope_ref, bf16[16,6144]{1,0:T(8,128)(2,1)S(1)} %collective-permute-done.4.refs_0_, bf16[16,6144]{1,0:T(8,128)(2,1)S(1)} %collective-permute-done.5.refs_1_, ...), custom_call_target="tpu_custom_call" | custom-call | tf_op jit(solution)/shard_map/total/pallas_call | solution.py:260
  (1 shorter events, 0.0 us)
Async XLA Ops:
  0.6 9.8 %collective-permute-start = (bf16[8,3072]{1,0:T(8,128)(2,1)}, bf16[8,3072]{1,0:T(8,128)(2,1)S(1)}, u32[]{:S(2)}, u32[]{:S(2)}) collective-permute-start(bf16[8,3072]{1,0:T(8,128)(2,1)} %g_hbm.1), channel_id=1, source_target_pairs={{0,8},{4,12},{8,0},{12,4},{16,24},{20,28},{24,16},{28,20},{1,9},{5... | collective-permute-start | bytes 147464 | tf_op jit(solution)/shard_map/ppermute | solution.py:272
  3.7 6.7 %collective-permute-start.2 = (bf16[8,3072]{1,0:T(8,128)(2,1)}, bf16[8,3072]{1,0:T(8,128)(2,1)S(1)}, u32[]{:S(2)}, u32[]{:S(2)}) collective-permute-start(bf16[8,3072]{1,0:T(8,128)(2,1)} %g_hbm.1), channel_id=1, source_target_pairs={{0,24},{4,28},{8,16},{12,20},{16,8},{20,12},{24,0},{28,4},{1,25},{... | collective-permute-start | bytes 147464 | tf_op jit(solution)/shard_map/ppermute | solution.py:272
  6.2 5.7 %collective-permute-start.1 = (bf16[8,3072]{1,0:T(8,128)(2,1)}, bf16[8,3072]{1,0:T(8,128)(2,1)S(1)}, u32[]{:S(2)}, u32[]{:S(2)}) collective-permute-start(bf16[8,3072]{1,0:T(8,128)(2,1)} %g_hbm.1), channel_id=1, source_target_pairs={{0,16},{4,20},{8,24},{12,28},{16,0},{20,4},{24,8},{28,12},{1,17},{... | collective-permute-start | bytes 147464 | tf_op jit(solution)/shard_map/ppermute | solution.py:272
  12.0 1.5 %collective-permute-start.3 = (bf16[32,3072]{1,0:T(8,128)(2,1)S(1)}, bf16[32,3072]{1,0:T(8,128)(2,1)S(1)}, u32[]{:S(2)}, u32[]{:S(2)}) collective-permute-start(bf16[32,3072]{1,0:T(8,128)(2,1)S(1)} %join.1.refs_0_), channel_id=1, source_target_pairs={{0,4},{4,0},{8,12},{12,8},{16,20},{20,16},{24,28},{28,24},{1,5},{5... | collective-permute-start | bytes 589832 | tf_op jit(solution)/shard_map/ppermute | solution.py:272
  25.6 16.5 %collective-permute-start.4 = (bf16[16,6144]{1,0:T(8,128)(2,1)S(1)}, bf16[16,6144]{1,0:T(8,128)(2,1)S(1)}, u32[]{:S(2)}, u32[]{:S(2)}) collective-permute-start(bf16[16,6144]{1,0:T(8,128)(2,1)S(1)} %get-tuple-element.15), channel_id=1, source_target_pairs={{0,1},{1,0},{2,3},{3,2},{4,5},{5,4},{6,7},{7,6},{8,9},{9,8},{10,11... | collective-permute-start | bytes 589832 | tf_op jit(solution)/shard_map/ppermute | solution.py:272
  27.2 15.0 %collective-permute-start.5 = (bf16[16,6144]{1,0:T(8,128)(2,1)S(1)}, bf16[16,6144]{1,0:T(8,128)(2,1)S(1)}, u32[]{:S(2)}, u32[]{:S(2)}) collective-permute-start(bf16[16,6144]{1,0:T(8,128)(2,1)S(1)} %get-tuple-element.16), channel_id=1, source_target_pairs={{0,2},{1,3},{2,0},{3,1},{4,6},{5,7},{6,4},{7,5},{8,10},{9,11},{10,... | collective-permute-start | bytes 589832 | tf_op jit(solution)/shard_map/ppermute | solution.py:272
  28.7 13.5 %collective-permute-start.6 = (bf16[16,6144]{1,0:T(8,128)(2,1)S(1)}, bf16[16,6144]{1,0:T(8,128)(2,1)S(1)}, u32[]{:S(2)}, u32[]{:S(2)}) collective-permute-start(bf16[16,6144]{1,0:T(8,128)(2,1)S(1)} %get-tuple-element.17), channel_id=1, source_target_pairs={{0,3},{1,2},{2,1},{3,0},{4,7},{5,6},{6,5},{7,4},{8,11},{9,10},{10,... | collective-permute-start | bytes 589832 | tf_op jit(solution)/shard_map/ppermute | solution.py:272

commit v4 on v3

--- a/solution.py
+++ b/solution.py
@@ -51,9 +51,12 @@
 
 
 VMEM = pltpu.VMEM
-CHUNKS = 12
-EARLY = 3
-GROUPS = 3
+UNITS = 2
+SIDE = 256
+ROWS = 3 * SIDE * UNITS
+SPLIT = 4
+MORE = 2
+BLOCKS = 24
 
 
 def in_vmem():
@@ -64,20 +67,28 @@
     return pl.BlockSpec(memory_space=pl.ANY)
 
 
+def in_hbm(value):
+    return pltpu.with_memory_space_constraint(value, pltpu.HBM)
+
+
 def params(mib):
     return pltpu.CompilerParams(vmem_limit_bytes=mib * 1024 * 1024)
 
 
-def gelu_kernel(parts, early, x_hbm, g_hbm, w_hbm, hidden_ref, slope_ref, own_ref, w_ref, x_ref, sems):
+def piece_of(w_hbm, i):
+    rows = pl.ds(pl.multiple_of((i // SPLIT) * ROWS, ROWS), ROWS)
+    wide = w_hbm.shape[1] // SPLIT
+    return w_hbm.at[rows, pl.ds(pl.multiple_of((i % SPLIT) * wide, wide), wide)]
+
+
+def gelu_kernel(parts, x_hbm, g_hbm, w_hbm, hidden_ref, slope_ref, own_ref, w_ref, x_ref, sems):
     bring_x = pltpu.make_async_copy(x_hbm, x_ref, sems.at[0])
     bring_g = pltpu.make_async_copy(g_hbm, own_ref, sems.at[1])
     bring_x.start()
     bring_g.start()
-    step = w_ref.shape[0] // early
-    bring_w = []
-    for i in range(early):
-        rows = pl.ds(i * step, step)
-        bring_w.append(pltpu.make_async_copy(w_hbm.at[rows], w_ref.at[rows], sems.at[2 + i]))
+    bring_w = [
+        pltpu.make_async_copy(piece_of(w_hbm, i), w_ref.at[i], sems.at[2 + i]) for i in range(SPLIT)
+    ]
     for copy in bring_w:
         copy.start()
     bring_x.wait()
@@ -95,27 +106,31 @@
         copy.wait()
 
 
-def gelu_call(parts, early, x, g, weight):
+def gelu_call(parts, x, g, weight):
     tokens, width = x.shape
     return pl.pallas_call(
-        functools.partial(gelu_kernel, parts, early),
+        functools.partial(gelu_kernel, parts),
         out_shape=(
             jax.ShapeDtypeStruct((tokens, width), BF16),
             jax.ShapeDtypeStruct((tokens // parts, width), F32),
             jax.ShapeDtypeStruct(g.shape, BF16),
-            jax.ShapeDtypeStruct((weight.shape[0] * early // CHUNKS, weight.shape[1]), BF16),
+            jax.ShapeDtypeStruct((SPLIT, ROWS, weight.shape[1] // SPLIT), BF16),
         ),
         in_specs=[pl.BlockSpec(memory_space=pltpu.HBM)] * 3,
         out_specs=(in_vmem(),) * 4,
-        scratch_shapes=[VMEM((tokens, width), BF16), pltpu.SemaphoreType.DMA((2 + early,))],
+        scratch_shapes=[VMEM((tokens, width), BF16), pltpu.SemaphoreType.DMA((2 + SPLIT,))],
         compiler_params=params(8),
         cost_estimate=pl.CostEstimate(
             flops=tokens * width * 20,
             transcendentals=tokens * width,
-            bytes_accessed=4 * tokens * width + weight.size * 2 * early // CHUNKS,
+            bytes_accessed=4 * tokens * width + 2 * ROWS * weight.shape[1],
         ),
         name="gelu",
-    )(*[pltpu.with_memory_space_constraint(v, pltpu.HBM) for v in (x, g, weight)])
+    )(in_hbm(x), in_hbm(g), in_hbm(weight))
+
+
+def tokens_padded(tokens):
+    return -(-tokens // 128) * 128
 
 
 def join_kernel(*refs):
@@ -136,17 +151,40 @@
     )(*blocks)
 
 
-def hidden_grad_kernel(n, parts, early, groups, *refs):
-    near_ref, swap_ref, w_hbm, held_ref = refs[:4]
-    g_out, own_out = refs[4:6]
-    sends = refs[6 : 6 + parts - 1]
-    w_ref, g_buf, sems = refs[6 + parts - 1 :]
-    late = CHUNKS - early
-    step = w_ref.shape[0] // late
+def fetch_kernel(near_ref, w_hbm, more_ref, sems):
+    copies = [
+        pltpu.make_async_copy(piece_of(w_hbm, SPLIT + i), more_ref.at[i], sems.at[i]) for i in range(MORE)
+    ]
+    for copy in copies:
+        copy.start()
+    for copy in copies:
+        copy.wait()
+
+
+def fetch_call(near, weight):
+    wide = weight.shape[1] // SPLIT
+    return pl.pallas_call(
+        fetch_kernel,
+        out_shape=jax.ShapeDtypeStruct((MORE, ROWS, wide), BF16),
+        in_specs=[in_vmem(), anywhere()],
+        out_specs=in_vmem(),
+        scratch_shapes=[pltpu.SemaphoreType.DMA((MORE,))],
+        compiler_params=params(2),
+        cost_estimate=pl.CostEstimate(flops=0, transcendentals=0, bytes_accessed=2 * MORE * ROWS * wide),
+        name="fetch",
+    )(near, in_hbm(weight))
+
+
+def hidden_grad_kernel(n, parts, *refs):
+    near_ref, swap_ref, w_hbm, held_ref, more_ref = refs[:5]
+    g_out, own_out = refs[5:7]
+    sends = refs[7 : 7 + parts - 1]
+    w_ref, columns_ref, g_buf, sems = refs[7 + parts - 1 :]
+    first = SPLIT + MORE
+    late = w_ref.shape[0]
 
     def bring(i):
-        source = w_hbm.at[pl.ds(pl.multiple_of((early + i) * step, step), step)]
-        return pltpu.make_async_copy(source, w_ref.at[pl.ds(pl.multiple_of(i * step, step), step)], sems.at[i])
+        return pltpu.make_async_copy(piece_of(w_hbm, first + i), w_ref.at[i], sems.at[i])
 
     for i in range(late):
         bring(i).start()
@@ -164,46 +202,91 @@
         g_buf[place(2 * j)] = near_ref[j * rows : (j + 1) * rows]
         g_buf[place(2 * j + 1)] = swap_ref[j * rows : (j + 1) * rows]
     g_out[...] = g_buf[...].reshape(g_out.shape)
-    share = n * rows // parts
-
-    def multiply(w, at):
-        part = contract_cols(w, g_out[...]).T
-        own_out[:, pl.ds(at, step)] = part[:share]
-        for k in range(1, parts):
-            sends[k - 1][:, pl.ds(at, step)] = part[k * share : (k + 1) * share].astype(BF16)
-
-    for j in range(early):
-        multiply(held_ref[j * step : (j + 1) * step], j * step)
-    each = late // groups
-
-    def group(i, unused):
-        for j in range(each):
-            bring(i * each + j).wait()
-        for j in range(each):
-            at = pl.multiple_of((i * each + j) * step, step)
-            multiply(w_ref[pl.ds(at, step)], pl.multiple_of(at + early * step, step))
-        return unused
-
-    lax.fori_loop(0, groups, group, 0)
-
-
-def hidden_grad_call(n, parts, early, groups, near, swap, weight, held):
-    width = near.shape[1]
+    tokens, width = g_out.shape
+    columns_ref[:, :tokens] = g_out[...].T
+    columns_ref[:, tokens:] = jnp.zeros_like(columns_ref[:, tokens:])
+    share = tokens // parts
+    block = 3 * SIDE
+    steps = width // SIDE
+    per_piece = steps // SPLIT
+
+    def run(*accs):
+        def hold_tokens(k):
+            for m in range(UNITS):
+                pltpu.matmul_push_rhs(columns_ref[pl.ds(pl.multiple_of(k * SIDE, SIDE), SIDE)], 0, m)
+
+        def multiply(ref, part, last=False):
+            for j in range(per_piece):
+                k = part * per_piece + j
+                here = slice(j * SIDE, (j + 1) * SIDE)
+                for m in range(UNITS):
+                    pltpu.matmul_acc_lhs(
+                        accs[2 * m + 1], ref[m * block + SIDE : (m + 1) * block, here], load_staged_rhs=0
+                    )
+                for m in range(UNITS):
+                    pltpu.matmul_push_rhs(ref[m * block : m * block + SIDE, here], 1, m, transpose=True)
+                if not (last and j == per_piece - 1):
+                    hold_tokens((k + 1) % steps)
+                depth = pl.ds(pl.multiple_of(k * SIDE, SIDE), SIDE)
+                for m in range(UNITS):
+                    pltpu.matmul_acc_lhs(accs[2 * m], g_out[:, depth], load_staged_rhs=1)
+
+        def store(part, at):
+            columns = pl.ds(at, part.shape[1])
+            own_out[:, columns] = part[:share]
+            for k in range(1, parts):
+                sends[k - 1][:, columns] = part[k * share : (k + 1) * share].astype(BF16)
+
+        def finish(at):
+            for m in range(UNITS):
+                start = pl.multiple_of(at + m * block, SIDE)
+                store(pltpu.matmul_pop(accs[2 * m]), start)
+                streamed = pltpu.matmul_pop(accs[2 * m + 1])[:, : tokens_padded(tokens)]
+                store(streamed.T[:tokens], pl.multiple_of(start + SIDE, SIDE))
+
+        hold_tokens(0)
+        for i in range(SPLIT):
+            multiply(held_ref.at[i], i)
+        finish(0)
+        for i in range(MORE):
+            multiply(more_ref.at[i], i)
+
+        def piece(i, unused):
+            bring(i).wait()
+            at = first + i
+            multiply(w_ref.at[i], at % SPLIT)
+
+            @pl.when(at % SPLIT == SPLIT - 1)
+            def _():
+                finish((at // SPLIT) * ROWS)
+
+            return unused
+
+        lax.fori_loop(0, late - 1, piece, 0)
+        bring(late - 1).wait()
+        multiply(w_ref.at[late - 1], SPLIT - 1, last=True)
+        finish(((first + late - 1) // SPLIT) * ROWS)
+
+    pl.run_scoped(run, *[pltpu.ACC(m)((size, SIDE), F32) for m in range(UNITS) for size in (tokens, 2 * SIDE)])
+
+
+def hidden_grad_call(n, parts, near, swap, weight, held, more):
+    ff, width = weight.shape
     tokens = 2 * near.shape[0]
-    ff = weight.shape[0]
     share = tokens // parts
-    late = CHUNKS - early
+    late = ff // ROWS * SPLIT - SPLIT - MORE
     outs = pl.pallas_call(
-        functools.partial(hidden_grad_kernel, n, parts, early, groups),
+        functools.partial(hidden_grad_kernel, n, parts),
         out_shape=(
             jax.ShapeDtypeStruct((tokens, width), BF16),
             jax.ShapeDtypeStruct((share, ff), F32),
             *[jax.ShapeDtypeStruct((share, ff), BF16)] * (parts - 1),
         ),
-        in_specs=[in_vmem()] * 2 + [anywhere(), in_vmem()],
-        out_specs=tuple([in_vmem()] * (parts + 1)),
+        in_specs=[in_vmem()] * 2 + [anywhere()] + [in_vmem()] * 2,
+        out_specs=(in_vmem(),) * (parts + 1),
         scratch_shapes=[
-            VMEM((ff * late // CHUNKS, width), BF16),
+            VMEM((late, ROWS, width // SPLIT), BF16),
+            VMEM((width, SIDE), BF16),
             VMEM((n, tokens // n, width), BF16),
             pltpu.SemaphoreType.DMA((late,)),
         ],
@@ -212,7 +295,7 @@
             flops=2 * tokens * width * ff, transcendentals=0, bytes_accessed=2 * width * ff
         ),
         name="hidden_grad",
-    )(near, swap, weight, held)
+    )(near, swap, in_hbm(weight), held, more)
     return outs[0], outs[1], outs[2:]
 
 
@@ -233,8 +316,7 @@
 def weight_grad_call(hidden, g):
     tokens, ff = hidden.shape
     width = g.shape[1]
-    step = ff // CHUNKS
-    sizes = [step // 2] * (2 * CHUNKS)
+    sizes = [ff // BLOCKS] * BLOCKS
     return pl.pallas_call(
         functools.partial(weight_grad_kernel, sizes),
         out_shape=jax.ShapeDtypeStruct((ff, width), BF16),
@@ -272,10 +354,11 @@
         return lax.ppermute(value, axis, [(i, i ^ k) for i in range(size)])
 
     far = [swap(grad_out, "hid", n, k) for k in range(n - 2, 0, -2)][::-1]
-    hidden, slope, own_rows, held = gelu_call(parts, EARLY, pre_act, grad_out, weight)
+    hidden, slope, own_rows, held = gelu_call(parts, pre_act, grad_out, weight)
     near = join_call([own_rows, *far])
     other = swap(near, "hid", n, 1)
-    g, own, sends = hidden_grad_call(n, parts, EARLY, GROUPS, near, other, weight, held)
+    more = fetch_call(near, weight)
+    g, own, sends = hidden_grad_call(n, parts, near, other, weight, held, more)
     received = [swap(s, "wid", parts, k + 1) for k, s in enumerate(sends)]
     grad_w = weight_grad_call(hidden, g)
     return (sum_call(own, slope, received), grad_w)
@@ -291,7 +374,8 @@
     def local(grad_out, pre_act, weight):
         ff, width = weight.shape
         small = power_of_two(n) and power_of_two(parts) and parts < n <= 8
-        if small and ff % (CHUNKS * 256) == 0 and width % 256 == 0 and ff * width * 2 <= 40 * 2**20:
+        fits = ff % ROWS == 0 and ff >= 2 * ROWS and ff % (BLOCKS * 128) == 0 and width % (SPLIT * SIDE) == 0
+        if small and fits and ff * width * 2 <= 40 * 2**20:
             return ring(n, parts, grad_out, pre_act, weight)
         return plain(grad_out, pre_act, weight)
 

time: 43.1 us -> 40.9 us (0.949)
  waiting for transfers between devices: 2.98 us -> 1.5 us
  Pallas kernels: 29.9 us -> 29.2 us
    ppermute x7, waiting for transfers between devices: 2.98 us -> 1.5 us  [swap(): return lax.ppermute(value, axis, [(i, i ^ k) for i in range(size)])]
    pallas_call x2 -> x3, Pallas kernels: 16.2 us -> 15.5 us  [the longest x1 8.94 us: hidden_grad_call(): pl.pallas_call(functools.partial(hidden_grad_kernel, n, parts), out_shape...]
  transfers between devices with their start and end apart: 7 -> 7, of which waited for: 3 -> 1; matrix products, arithmetic and copies ran while one was open for 0% -> 0% of each run, Pallas kernels for 40% -> 48%
where the time goes in v4:
time: 40.9 us; the launch traced here: 40.7 us
  Pallas kernels  29.2 us (71%)
  starting transfers between devices  9.33 us (23%)
  waiting for transfers between devices  1.5 us (4%)
  between operations  0.72 us (2%)
    pallas_call x1, Pallas kernels, weight_grad_call(): pl.pallas_call(functools.partial(weight_grad_kernel, sizes), out_shape=ja...  12.9 us
    ppermute x7, starting transfers between devices, swap(): return lax.ppermute(value, axis, [(i, i ^ k) for i in range(size)])  9.33 us
    pallas_call x1, Pallas kernels, hidden_grad_call(): pl.pallas_call(functools.partial(hidden_grad_kernel, n, parts), out_shape...  8.94 us
    pallas_call x1, Pallas kernels, gelu_call(): pl.pallas_call(functools.partial(gelu_kernel, parts), out_shape=(jax.Shap...  4.1 us
    pallas_call x1, Pallas kernels, fetch_call(): pl.pallas_call(fetch_kernel, out_shape=jax.ShapeDtypeStruct((MORE, ROWS,...  2.41 us
    ppermute x7, waiting for transfers between devices, swap(): return lax.ppermute(value, axis, [(i, i ^ k) for i in range(size)])  1.5 us
  transfers between devices with their start and end apart: 7, of which 1 were waited for; matrix products, arithmetic and copies ran while one was open for 0% of the time, Pallas kernels for 48%

profile of v4, /device:TPU:0, one launch (start us, length us, event | category | flops | bytes accessed | tf_op | source)
XLA Modules:
  0.0 40.7 jit_solution(9598509474593765856)
XLA Ops:
  0.6 3.1 %collective-permute-start = (bf16[8,3072]{1,0:T(8,128)(2,1)}, bf16[8,3072]{1,0:T(8,128)(2,1)S(1)}, u32[]{:S(2)}, u32[]{:S(2)}) collective-permute-start(bf16[8,3072]{1,0:T(8,128)(2,1)} %g_hbm.1), channel_id=1, source_target_pairs={{0,8},{4,12},{8,0},{12,4},{16,24},{20,28},{24,16},{28,20},{1,9},{5... | collective-permute-start | bytes 147464 | tf_op jit(solution)/shard_map/ppermute | solution.py:354
  3.7 2.5 %collective-permute-start.2 = (bf16[8,3072]{1,0:T(8,128)(2,1)}, bf16[8,3072]{1,0:T(8,128)(2,1)S(1)}, u32[]{:S(2)}, u32[]{:S(2)}) collective-permute-start(bf16[8,3072]{1,0:T(8,128)(2,1)} %g_hbm.1), channel_id=1, source_target_pairs={{0,24},{4,28},{8,16},{12,20},{16,8},{20,12},{24,0},{28,4},{1,25},{... | collective-permute-start | bytes 147464 | tf_op jit(solution)/shard_map/ppermute | solution.py:354
  6.2 0.1 collective-permute-start.1
  6.3 4.1 %gelu.1 = (bf16[64,6144]{1,0:T(8,128)(2,1)S(1)}, f32[16,6144]{1,0:T(8,128)S(1)}, bf16[8,3072]{1,0:T(8,128)(2,1)S(1)}, bf16[4,1536,768]{2,1,0:T(8,128)(2,1)S(1)}) custom-call(bf16[64,6144]{1,0:T(8,128)(2,1)} %x_hbm.1, bf16[8,3072]{1,0:T(8,128)(2,1)} %g_hbm.1, bf16[6144,3072]{1,0:T(8,128)(2,1)} %refs_2_.1), custom_call_target="tpu_custom_call" | custom-call | flops 7864320 | bytes 11010048 | tf_op jit(solution)/shard_map/gelu/pallas_call | solution.py:111
  10.5 0.0 collective-permute-done.refs_1_
  10.5 0.0 collective-permute-done.2.refs_3_
  10.5 1.5 %collective-permute-done.1.refs_2_ = bf16[8,3072]{1,0:T(8,128)(2,1)S(1)} collective-permute-done((bf16[8,3072]{1,0:T(8,128)(2,1)}, bf16[8,3072]{1,0:T(8,128)(2,1)S(1)}, u32[]{:S(2)}, u32[]{:S(2)}) %collective-permute-start.1) | collective-permute-done | bytes 49184 | tf_op jit(solution)/shard_map/ppermute | solution.py:354
  12.0 0.1 collective-permute-start.3
  12.0 2.4 %fetch.1.refs_4_ = bf16[2,1536,768]{2,1,0:T(8,128)(2,1)S(1)} custom-call(bf16[32,3072]{1,0:T(8,128)(2,1)S(1)} %join.1.near_ref.refs_0_, bf16[6144,3072]{1,0:T(8,128)(2,1)} %refs_2_.1), custom_call_target="tpu_custom_call" | custom-call | bytes 4718592 | tf_op jit(solution)/shard_map/fetch/pallas_call | solution.py:166
  14.5 0.0 collective-permute-done.3.refs_1_
  14.5 8.9 %hidden_grad.1 = (bf16[64,3072]{1,0:T(8,128)(2,1)S(1)}, f32[16,6144]{1,0:T(8,128)S(1)}, bf16[16,6144]{1,0:T(8,128)(2,1)S(1)}, bf16[16,6144]{1,0:T(8,128)(2,1)S(1)}, bf16[16,6144]{1,0:T(8,128)(2,1)S(1)}) custom-call(bf16[32,3072]{1,0:T(8,128)(2,1)S(1)} %join.1.near_ref.refs_0_, bf16[32,3072]{1,0:T(8,128)(2,1)S(1)} %collective-permute-done.3.refs_1_, ...), custom_call_target="tpu_custom_call" | custom-call | flops 2415919104 | bytes 37748736 | tf_op jit(solution)/shard_map/hidden_grad/pallas_call | solution.py:278
  23.4 1.6 %collective-permute-start.4 = (bf16[16,6144]{1,0:T(8,128)(2,1)S(1)}, bf16[16,6144]{1,0:T(8,128)(2,1)S(1)}, u32[]{:S(2)}, u32[]{:S(2)}) collective-permute-start(bf16[16,6144]{1,0:T(8,128)(2,1)S(1)} %get-tuple-element.15), channel_id=1, source_target_pairs={{0,1},{1,0},{2,3},{3,2},{4,5},{5,4},{6,7},{7,6},{8,9},{9,8},{10,11... | collective-permute-start | bytes 589832 | tf_op jit(solution)/shard_map/ppermute | solution.py:354
  25.0 1.5 %collective-permute-start.5 = (bf16[16,6144]{1,0:T(8,128)(2,1)S(1)}, bf16[16,6144]{1,0:T(8,128)(2,1)S(1)}, u32[]{:S(2)}, u32[]{:S(2)}) collective-permute-start(bf16[16,6144]{1,0:T(8,128)(2,1)S(1)} %get-tuple-element.16), channel_id=1, source_target_pairs={{0,2},{1,3},{2,0},{3,1},{4,6},{5,7},{6,4},{7,5},{8,10},{9,11},{10,... | collective-permute-start | bytes 589832 | tf_op jit(solution)/shard_map/ppermute | solution.py:354
  26.5 0.5 %collective-permute-start.6 = (bf16[16,6144]{1,0:T(8,128)(2,1)S(1)}, bf16[16,6144]{1,0:T(8,128)(2,1)S(1)}, u32[]{:S(2)}, u32[]{:S(2)}) collective-permute-start(bf16[16,6144]{1,0:T(8,128)(2,1)S(1)} %get-tuple-element.17), channel_id=1, source_target_pairs={{0,3},{1,2},{2,1},{3,0},{4,7},{5,6},{6,5},{7,4},{8,11},{9,10},{10,... | collective-permute-start | bytes 589832 | tf_op jit(solution)/shard_map/ppermute | solution.py:354
  27.0 12.9 %weight_grad.1 = bf16[6144,3072]{1,0:T(8,128)(2,1)} custom-call(bf16[64,6144]{1,0:T(8,128)(2,1)S(1)} %get-tuple-element.18.hidden_ref, bf16[64,3072]{1,0:T(8,128)(2,1)S(1)} %get-tuple-element.19.g_ref), custom_call_target="tpu_custom_call" | custom-call | flops 2415919104 | bytes 37748736 | tf_op jit(solution)/shard_map/weight_grad/pallas_call | solution.py:320
  39.9 0.0 collective-permute-done.4.refs_0_
  39.9 0.0 collective-permute-done.5.refs_1_
  40.0 0.0 collective-permute-done.6.refs_2_
  40.0 0.8 %total.1 = bf16[16,6144]{1,0:T(8,128)(2,1)} custom-call(f32[16,6144]{1,0:T(8,128)S(1)} %get-tuple-element.13.own_ref, f32[16,6144]{1,0:T(8,128)S(1)} %get-tuple-element.14.slope_ref, bf16[16,6144]{1,0:T(8,128)(2,1)S(1)} %collective-permute-done.4.refs_0_, bf16[16,6144]{1,0:T(8,128)(2,1)S(1)} %collective-permute-done.5.refs_1_, ...), custom_call_target="tpu_custom_call" | custom-call | tf_op jit(solution)/shard_map/total/pallas_call | solution.py:342
  (1 shorter events, 0.0 us)
Async XLA Ops:
  0.6 9.8 %collective-permute-start = (bf16[8,3072]{1,0:T(8,128)(2,1)}, bf16[8,3072]{1,0:T(8,128)(2,1)S(1)}, u32[]{:S(2)}, u32[]{:S(2)}) collective-permute-start(bf16[8,3072]{1,0:T(8,128)(2,1)} %g_hbm.1), channel_id=1, source_target_pairs={{0,8},{4,12},{8,0},{12,4},{16,24},{20,28},{24,16},{28,20},{1,9},{5... | collective-permute-start | bytes 147464 | tf_op jit(solution)/shard_map/ppermute | solution.py:354
  3.7 6.7 %collective-permute-start.2 = (bf16[8,3072]{1,0:T(8,128)(2,1)}, bf16[8,3072]{1,0:T(8,128)(2,1)S(1)}, u32[]{:S(2)}, u32[]{:S(2)}) collective-permute-start(bf16[8,3072]{1,0:T(8,128)(2,1)} %g_hbm.1), channel_id=1, source_target_pairs={{0,24},{4,28},{8,16},{12,20},{16,8},{20,12},{24,0},{28,4},{1,25},{... | collective-permute-start | bytes 147464 | tf_op jit(solution)/shard_map/ppermute | solution.py:354
  6.2 5.7 %collective-permute-start.1 = (bf16[8,3072]{1,0:T(8,128)(2,1)}, bf16[8,3072]{1,0:T(8,128)(2,1)S(1)}, u32[]{:S(2)}, u32[]{:S(2)}) collective-permute-start(bf16[8,3072]{1,0:T(8,128)(2,1)} %g_hbm.1), channel_id=1, source_target_pairs={{0,16},{4,20},{8,24},{12,28},{16,0},{20,4},{24,8},{28,12},{1,17},{... | collective-permute-start | bytes 147464 | tf_op jit(solution)/shard_map/ppermute | solution.py:354
  12.0 2.5 %collective-permute-start.3 = (bf16[32,3072]{1,0:T(8,128)(2,1)S(1)}, bf16[32,3072]{1,0:T(8,128)(2,1)S(1)}, u32[]{:S(2)}, u32[]{:S(2)}) collective-permute-start(bf16[32,3072]{1,0:T(8,128)(2,1)S(1)} %join.1.near_ref.refs_0_), channel_id=1, source_target_pairs={{0,4},{4,0},{8,12},{12,8},{16,20},{20,16},{24,28},{28,24},{1,5},{5... | collective-permute-start | bytes 589832 | tf_op jit(solution)/shard_map/ppermute | solution.py:354
  23.4 16.5 %collective-permute-start.4 = (bf16[16,6144]{1,0:T(8,128)(2,1)S(1)}, bf16[16,6144]{1,0:T(8,128)(2,1)S(1)}, u32[]{:S(2)}, u32[]{:S(2)}) collective-permute-start(bf16[16,6144]{1,0:T(8,128)(2,1)S(1)} %get-tuple-element.15), channel_id=1, source_target_pairs={{0,1},{1,0},{2,3},{3,2},{4,5},{5,4},{6,7},{7,6},{8,9},{9,8},{10,11... | collective-permute-start | bytes 589832 | tf_op jit(solution)/shard_map/ppermute | solution.py:354
  25.0 15.0 %collective-permute-start.5 = (bf16[16,6144]{1,0:T(8,128)(2,1)S(1)}, bf16[16,6144]{1,0:T(8,128)(2,1)S(1)}, u32[]{:S(2)}, u32[]{:S(2)}) collective-permute-start(bf16[16,6144]{1,0:T(8,128)(2,1)S(1)} %get-tuple-element.16), channel_id=1, source_target_pairs={{0,2},{1,3},{2,0},{3,1},{4,6},{5,7},{6,4},{7,5},{8,10},{9,11},{10,... | collective-permute-start | bytes 589832 | tf_op jit(solution)/shard_map/ppermute | solution.py:354
  26.5 13.5 %collective-permute-start.6 = (bf16[16,6144]{1,0:T(8,128)(2,1)S(1)}, bf16[16,6144]{1,0:T(8,128)(2,1)S(1)}, u32[]{:S(2)}, u32[]{:S(2)}) collective-permute-start(bf16[16,6144]{1,0:T(8,128)(2,1)S(1)} %get-tuple-element.17), channel_id=1, source_target_pairs={{0,3},{1,2},{2,1},{3,0},{4,7},{5,6},{6,5},{7,4},{8,11},{9,10},{10,... | collective-permute-start | bytes 589832 | tf_op jit(solution)/shard_map/ppermute | solution.py:354

commit v5 on v4

--- a/solution.py
+++ b/solution.py
@@ -7,6 +7,7 @@
 from jax.experimental import pallas as pl
 from jax.experimental.pallas import tpu as pltpu
 from jax.sharding import PartitionSpec as P
+
 
 coef = math.sqrt(2.0 / math.pi)
 BF16 = jnp.bfloat16
@@ -36,7 +37,7 @@
 
 
 def plain(grad_out, pre_act, weight):
-    value, unused = gelu_parts(pre_act.astype(F32))
+    value, _ = gelu_parts(pre_act.astype(F32))
     hidden = value.astype(BF16)
     gathered = lax.all_gather(grad_out, "hid", axis=0, tiled=True)
     grad_w = contract_rows(hidden, gathered)
@@ -45,7 +46,7 @@
     own_rows = share.shape[0]
     offset = lax.axis_index("wid") * own_rows
     local_pre = lax.dynamic_slice_in_dim(pre_act, offset, own_rows, 0)
-    unused_value, slope = gelu_parts(local_pre.astype(F32))
+    _, slope = gelu_parts(local_pre.astype(F32))
     grad_pre = (share * slope).astype(BF16)
     return (grad_pre, grad_w.astype(BF16))
 
@@ -179,7 +180,7 @@
     near_ref, swap_ref, w_hbm, held_ref, more_ref = refs[:5]
     g_out, own_out = refs[5:7]
     sends = refs[7 : 7 + parts - 1]
-    w_ref, columns_ref, g_buf, sems = refs[7 + parts - 1 :]
+    w_ref, columns_ref, sems = refs[7 + parts - 1 :]
     first = SPLIT + MORE
     late = w_ref.shape[0]
 
@@ -196,12 +197,11 @@
     def place(k):
         source = lax.bitwise_xor(hid, k)
         block = lax.bitwise_xor(source // per, wid)
-        return block * per + lax.rem(source, per)
+        return pl.multiple_of((block * per + lax.rem(source, per)) * rows, rows)
 
     for j in range(n // 2):
-        g_buf[place(2 * j)] = near_ref[j * rows : (j + 1) * rows]
-        g_buf[place(2 * j + 1)] = swap_ref[j * rows : (j + 1) * rows]
-    g_out[...] = g_buf[...].reshape(g_out.shape)
+        g_out[pl.ds(place(2 * j), rows)] = near_ref[j * rows : (j + 1) * rows]
+        g_out[pl.ds(place(2 * j + 1), rows)] = swap_ref[j * rows : (j + 1) * rows]
     tokens, width = g_out.shape
     columns_ref[:, :tokens] = g_out[...].T
     columns_ref[:, tokens:] = jnp.zeros_like(columns_ref[:, tokens:])
@@ -287,7 +287,6 @@
         scratch_shapes=[
             VMEM((late, ROWS, width // SPLIT), BF16),
             VMEM((width, SIDE), BF16),
-            VMEM((n, tokens // n, width), BF16),
             pltpu.SemaphoreType.DMA((late,)),
         ],
         compiler_params=params(32),
@@ -353,7 +352,9 @@
     def swap(value, axis, size, k):
         return lax.ppermute(value, axis, [(i, i ^ k) for i in range(size)])
 
-    far = [swap(grad_out, "hid", n, k) for k in range(n - 2, 0, -2)][::-1]
+    far = []
+    for k in range(2, n, 2):
+        far.append(swap(grad_out, "hid", n, k))
     hidden, slope, own_rows, held = gelu_call(parts, pre_act, grad_out, weight)
     near = join_call([own_rows, *far])
     other = swap(near, "hid", n, 1)

time: 40.9 us -> 40.9 us (level)
  no operation moved by 1% of the time
where the time goes in v5:
time: 40.9 us; the launch traced here: 40.7 us
  Pallas kernels  29.2 us (71%)
  starting transfers between devices  9.33 us (23%)
  waiting for transfers between devices  1.5 us (4%)
  between operations  0.72 us (2%)
    pallas_call x1, Pallas kernels, weight_grad_call(): pl.pallas_call(functools.partial(weight_grad_kernel, sizes), out_shape=ja...  12.9 us
    ppermute x7, starting transfers between devices, swap(): return lax.ppermute(value, axis, [(i, i ^ k) for i in range(size)])  9.33 us
    pallas_call x1, Pallas kernels, hidden_grad_call(): pl.pallas_call(functools.partial(hidden_grad_kernel, n, parts), out_shape...  8.94 us
    pallas_call x1, Pallas kernels, gelu_call(): pl.pallas_call(functools.partial(gelu_kernel, parts), out_shape=(jax.Shap...  4.1 us
    pallas_call x1, Pallas kernels, fetch_call(): pl.pallas_call(fetch_kernel, out_shape=jax.ShapeDtypeStruct((MORE, ROWS,...  2.41 us
    ppermute x7, waiting for transfers between devices, swap(): return lax.ppermute(value, axis, [(i, i ^ k) for i in range(size)])  1.5 us
  transfers between devices with their start and end apart: 7, of which 1 were waited for; matrix products, arithmetic and copies ran while one was open for 0% of the time, Pallas kernels for 48%

profile of v5, /device:TPU:0, one launch (start us, length us, event | category | flops | bytes accessed | tf_op | source)
XLA Modules:
  0.0 40.7 jit_solution(5133331804271977709)
XLA Ops:
  0.6 3.1 %collective-permute-start = (bf16[8,3072]{1,0:T(8,128)(2,1)}, bf16[8,3072]{1,0:T(8,128)(2,1)S(1)}, u32[]{:S(2)}, u32[]{:S(2)}) collective-permute-start(bf16[8,3072]{1,0:T(8,128)(2,1)} %g_hbm.1), channel_id=1, source_target_pairs={{0,8},{4,12},{8,0},{12,4},{16,24},{20,28},{24,16},{28,20},{1,9},{5... | collective-permute-start | bytes 147464 | tf_op jit(solution)/shard_map/ppermute | solution.py:353
  3.7 2.5 %collective-permute-start.2 = (bf16[8,3072]{1,0:T(8,128)(2,1)}, bf16[8,3072]{1,0:T(8,128)(2,1)S(1)}, u32[]{:S(2)}, u32[]{:S(2)}) collective-permute-start(bf16[8,3072]{1,0:T(8,128)(2,1)} %g_hbm.1), channel_id=1, source_target_pairs={{0,24},{4,28},{8,16},{12,20},{16,8},{20,12},{24,0},{28,4},{1,25},{... | collective-permute-start | bytes 147464 | tf_op jit(solution)/shard_map/ppermute | solution.py:353
  6.2 0.1 collective-permute-start.1
  6.3 4.1 %gelu.1 = (bf16[64,6144]{1,0:T(8,128)(2,1)S(1)}, f32[16,6144]{1,0:T(8,128)S(1)}, bf16[8,3072]{1,0:T(8,128)(2,1)S(1)}, bf16[4,1536,768]{2,1,0:T(8,128)(2,1)S(1)}) custom-call(bf16[64,6144]{1,0:T(8,128)(2,1)} %x_hbm.1, bf16[8,3072]{1,0:T(8,128)(2,1)} %g_hbm.1, bf16[6144,3072]{1,0:T(8,128)(2,1)} %refs_2_.1), custom_call_target="tpu_custom_call" | custom-call | flops 7864320 | bytes 11010048 | tf_op jit(solution)/shard_map/gelu/pallas_call | solution.py:112
  10.5 0.0 collective-permute-done.refs_1_
  10.5 0.0 collective-permute-done.2.refs_3_
  10.5 1.5 %collective-permute-done.1.refs_2_ = bf16[8,3072]{1,0:T(8,128)(2,1)S(1)} collective-permute-done((bf16[8,3072]{1,0:T(8,128)(2,1)}, bf16[8,3072]{1,0:T(8,128)(2,1)S(1)}, u32[]{:S(2)}, u32[]{:S(2)}) %collective-permute-start.1) | collective-permute-done | bytes 49184 | tf_op jit(solution)/shard_map/ppermute | solution.py:353
  12.0 0.1 collective-permute-start.3
  12.0 2.4 %fetch.1.refs_4_ = bf16[2,1536,768]{2,1,0:T(8,128)(2,1)S(1)} custom-call(bf16[32,3072]{1,0:T(8,128)(2,1)S(1)} %join.1.near_ref.refs_0_, bf16[6144,3072]{1,0:T(8,128)(2,1)} %refs_2_.1), custom_call_target="tpu_custom_call" | custom-call | bytes 4718592 | tf_op jit(solution)/shard_map/fetch/pallas_call | solution.py:167
  14.5 0.0 collective-permute-done.3.refs_1_
  14.5 8.9 %hidden_grad.1 = (bf16[64,3072]{1,0:T(8,128)(2,1)S(1)}, f32[16,6144]{1,0:T(8,128)S(1)}, bf16[16,6144]{1,0:T(8,128)(2,1)S(1)}, bf16[16,6144]{1,0:T(8,128)(2,1)S(1)}, bf16[16,6144]{1,0:T(8,128)(2,1)S(1)}) custom-call(bf16[32,3072]{1,0:T(8,128)(2,1)S(1)} %join.1.near_ref.refs_0_, bf16[32,3072]{1,0:T(8,128)(2,1)S(1)} %collective-permute-done.3.refs_1_, ...), custom_call_target="tpu_custom_call" | custom-call | flops 2415919104 | bytes 37748736 | tf_op jit(solution)/shard_map/hidden_grad/pallas_call | solution.py:278
  23.4 1.6 %collective-permute-start.4 = (bf16[16,6144]{1,0:T(8,128)(2,1)S(1)}, bf16[16,6144]{1,0:T(8,128)(2,1)S(1)}, u32[]{:S(2)}, u32[]{:S(2)}) collective-permute-start(bf16[16,6144]{1,0:T(8,128)(2,1)S(1)} %get-tuple-element.15), channel_id=1, source_target_pairs={{0,1},{1,0},{2,3},{3,2},{4,5},{5,4},{6,7},{7,6},{8,9},{9,8},{10,11... | collective-permute-start | bytes 589832 | tf_op jit(solution)/shard_map/ppermute | solution.py:353
  25.0 1.5 %collective-permute-start.5 = (bf16[16,6144]{1,0:T(8,128)(2,1)S(1)}, bf16[16,6144]{1,0:T(8,128)(2,1)S(1)}, u32[]{:S(2)}, u32[]{:S(2)}) collective-permute-start(bf16[16,6144]{1,0:T(8,128)(2,1)S(1)} %get-tuple-element.16), channel_id=1, source_target_pairs={{0,2},{1,3},{2,0},{3,1},{4,6},{5,7},{6,4},{7,5},{8,10},{9,11},{10,... | collective-permute-start | bytes 589832 | tf_op jit(solution)/shard_map/ppermute | solution.py:353
  26.5 0.5 %collective-permute-start.6 = (bf16[16,6144]{1,0:T(8,128)(2,1)S(1)}, bf16[16,6144]{1,0:T(8,128)(2,1)S(1)}, u32[]{:S(2)}, u32[]{:S(2)}) collective-permute-start(bf16[16,6144]{1,0:T(8,128)(2,1)S(1)} %get-tuple-element.17), channel_id=1, source_target_pairs={{0,3},{1,2},{2,1},{3,0},{4,7},{5,6},{6,5},{7,4},{8,11},{9,10},{10,... | collective-permute-start | bytes 589832 | tf_op jit(solution)/shard_map/ppermute | solution.py:353
  27.0 12.9 %weight_grad.1 = bf16[6144,3072]{1,0:T(8,128)(2,1)} custom-call(bf16[64,6144]{1,0:T(8,128)(2,1)S(1)} %get-tuple-element.18.hidden_ref, bf16[64,3072]{1,0:T(8,128)(2,1)S(1)} %get-tuple-element.19.g_ref), custom_call_target="tpu_custom_call" | custom-call | flops 2415919104 | bytes 37748736 | tf_op jit(solution)/shard_map/weight_grad/pallas_call | solution.py:319
  39.9 0.0 collective-permute-done.4.refs_0_
  39.9 0.0 collective-permute-done.5.refs_1_
  40.0 0.0 collective-permute-done.6.refs_2_
  40.0 0.8 %total.1 = bf16[16,6144]{1,0:T(8,128)(2,1)} custom-call(f32[16,6144]{1,0:T(8,128)S(1)} %get-tuple-element.13.own_ref, f32[16,6144]{1,0:T(8,128)S(1)} %get-tuple-element.14.slope_ref, bf16[16,6144]{1,0:T(8,128)(2,1)S(1)} %collective-permute-done.4.refs_0_, bf16[16,6144]{1,0:T(8,128)(2,1)S(1)} %collective-permute-done.5.refs_1_, ...), custom_call_target="tpu_custom_call" | custom-call | tf_op jit(solution)/shard_map/total/pallas_call | solution.py:341
  (1 shorter events, 0.0 us)
Async XLA Ops:
  0.6 9.8 %collective-permute-start = (bf16[8,3072]{1,0:T(8,128)(2,1)}, bf16[8,3072]{1,0:T(8,128)(2,1)S(1)}, u32[]{:S(2)}, u32[]{:S(2)}) collective-permute-start(bf16[8,3072]{1,0:T(8,128)(2,1)} %g_hbm.1), channel_id=1, source_target_pairs={{0,8},{4,12},{8,0},{12,4},{16,24},{20,28},{24,16},{28,20},{1,9},{5... | collective-permute-start | bytes 147464 | tf_op jit(solution)/shard_map/ppermute | solution.py:353
  3.7 6.7 %collective-permute-start.2 = (bf16[8,3072]{1,0:T(8,128)(2,1)}, bf16[8,3072]{1,0:T(8,128)(2,1)S(1)}, u32[]{:S(2)}, u32[]{:S(2)}) collective-permute-start(bf16[8,3072]{1,0:T(8,128)(2,1)} %g_hbm.1), channel_id=1, source_target_pairs={{0,24},{4,28},{8,16},{12,20},{16,8},{20,12},{24,0},{28,4},{1,25},{... | collective-permute-start | bytes 147464 | tf_op jit(solution)/shard_map/ppermute | solution.py:353
  6.2 5.7 %collective-permute-start.1 = (bf16[8,3072]{1,0:T(8,128)(2,1)}, bf16[8,3072]{1,0:T(8,128)(2,1)S(1)}, u32[]{:S(2)}, u32[]{:S(2)}) collective-permute-start(bf16[8,3072]{1,0:T(8,128)(2,1)} %g_hbm.1), channel_id=1, source_target_pairs={{0,16},{4,20},{8,24},{12,28},{16,0},{20,4},{24,8},{28,12},{1,17},{... | collective-permute-start | bytes 147464 | tf_op jit(solution)/shard_map/ppermute | solution.py:353
  12.0 2.5 %collective-permute-start.3 = (bf16[32,3072]{1,0:T(8,128)(2,1)S(1)}, bf16[32,3072]{1,0:T(8,128)(2,1)S(1)}, u32[]{:S(2)}, u32[]{:S(2)}) collective-permute-start(bf16[32,3072]{1,0:T(8,128)(2,1)S(1)} %join.1.near_ref.refs_0_), channel_id=1, source_target_pairs={{0,4},{4,0},{8,12},{12,8},{16,20},{20,16},{24,28},{28,24},{1,5},{5... | collective-permute-start | bytes 589832 | tf_op jit(solution)/shard_map/ppermute | solution.py:353
  23.4 16.5 %collective-permute-start.4 = (bf16[16,6144]{1,0:T(8,128)(2,1)S(1)}, bf16[16,6144]{1,0:T(8,128)(2,1)S(1)}, u32[]{:S(2)}, u32[]{:S(2)}) collective-permute-start(bf16[16,6144]{1,0:T(8,128)(2,1)S(1)} %get-tuple-element.15), channel_id=1, source_target_pairs={{0,1},{1,0},{2,3},{3,2},{4,5},{5,4},{6,7},{7,6},{8,9},{9,8},{10,11... | collective-permute-start | bytes 589832 | tf_op jit(solution)/shard_map/ppermute | solution.py:353
  25.0 15.0 %collective-permute-start.5 = (bf16[16,6144]{1,0:T(8,128)(2,1)S(1)}, bf16[16,6144]{1,0:T(8,128)(2,1)S(1)}, u32[]{:S(2)}, u32[]{:S(2)}) collective-permute-start(bf16[16,6144]{1,0:T(8,128)(2,1)S(1)} %get-tuple-element.16), channel_id=1, source_target_pairs={{0,2},{1,3},{2,0},{3,1},{4,6},{5,7},{6,4},{7,5},{8,10},{9,11},{10,... | collective-permute-start | bytes 589832 | tf_op jit(solution)/shard_map/ppermute | solution.py:353
  26.5 13.5 %collective-permute-start.6 = (bf16[16,6144]{1,0:T(8,128)(2,1)S(1)}, bf16[16,6144]{1,0:T(8,128)(2,1)S(1)}, u32[]{:S(2)}, u32[]{:S(2)}) collective-permute-start(bf16[16,6144]{1,0:T(8,128)(2,1)S(1)} %get-tuple-element.17), channel_id=1, source_target_pairs={{0,3},{1,2},{2,1},{3,0},{4,7},{5,6},{6,5},{7,4},{8,11},{9,10},{10,... | collective-permute-start | bytes 589832 | tf_op jit(solution)/shard_map/ppermute | solution.py:353

commit v6 on v5

--- a/solution.py
+++ b/solution.py
@@ -55,8 +55,9 @@
 UNITS = 2
 SIDE = 256
 ROWS = 3 * SIDE * UNITS
-SPLIT = 4
-MORE = 2
+SPLIT = 6
+EARLY = 7
+MORE = 1
 BLOCKS = 24
 
 
@@ -88,7 +89,7 @@
     bring_x.start()
     bring_g.start()
     bring_w = [
-        pltpu.make_async_copy(piece_of(w_hbm, i), w_ref.at[i], sems.at[2 + i]) for i in range(SPLIT)
+        pltpu.make_async_copy(piece_of(w_hbm, i), w_ref.at[i], sems.at[2 + i]) for i in range(EARLY)
     ]
     for copy in bring_w:
         copy.start()
@@ -115,16 +116,16 @@
             jax.ShapeDtypeStruct((tokens, width), BF16),
             jax.ShapeDtypeStruct((tokens // parts, width), F32),
             jax.ShapeDtypeStruct(g.shape, BF16),
-            jax.ShapeDtypeStruct((SPLIT, ROWS, weight.shape[1] // SPLIT), BF16),
+            jax.ShapeDtypeStruct((EARLY, ROWS, weight.shape[1] // SPLIT), BF16),
         ),
         in_specs=[pl.BlockSpec(memory_space=pltpu.HBM)] * 3,
         out_specs=(in_vmem(),) * 4,
-        scratch_shapes=[VMEM((tokens, width), BF16), pltpu.SemaphoreType.DMA((2 + SPLIT,))],
+        scratch_shapes=[VMEM((tokens, width), BF16), pltpu.SemaphoreType.DMA((2 + EARLY,))],
         compiler_params=params(8),
         cost_estimate=pl.CostEstimate(
             flops=tokens * width * 20,
             transcendentals=tokens * width,
-            bytes_accessed=4 * tokens * width + 2 * ROWS * weight.shape[1],
+            bytes_accessed=4 * tokens * width + 2 * ROWS * weight.shape[1] * EARLY // SPLIT,
         ),
         name="gelu",
     )(in_hbm(x), in_hbm(g), in_hbm(weight))
@@ -154,7 +155,7 @@
 
 def fetch_kernel(near_ref, w_hbm, more_ref, sems):
     copies = [
-        pltpu.make_async_copy(piece_of(w_hbm, SPLIT + i), more_ref.at[i], sems.at[i]) for i in range(MORE)
+        pltpu.make_async_copy(piece_of(w_hbm, EARLY + i), more_ref.at[i], sems.at[i]) for i in range(MORE)
     ]
     for copy in copies:
         copy.start()
@@ -181,7 +182,7 @@
     g_out, own_out = refs[5:7]
     sends = refs[7 : 7 + parts - 1]
     w_ref, columns_ref, sems = refs[7 + parts - 1 :]
-    first = SPLIT + MORE
+    first = EARLY + MORE
     late = w_ref.shape[0]
 
     def bring(i):
@@ -245,11 +246,23 @@
                 store(streamed.T[:tokens], pl.multiple_of(start + SIDE, SIDE))
 
         hold_tokens(0)
-        for i in range(SPLIT):
-            multiply(held_ref.at[i], i)
-        finish(0)
-        for i in range(MORE):
-            multiply(more_ref.at[i], i)
+
+        def held_piece(i, unused):
+            multiply(held_ref.at[i], i % SPLIT)
+
+            @pl.when(i == SPLIT - 1)
+            def _():
+                finish(0)
+
+            return unused
+
+        def more_piece(i, unused):
+            multiply(more_ref.at[i], (EARLY + i) % SPLIT)
+            return unused
+
+        extra = lax.shift_right_logical(hid, 16)
+        lax.fori_loop(0, EARLY + extra, held_piece, 0)
+        lax.fori_loop(0, MORE + extra, more_piece, 0)
 
         def piece(i, unused):
             bring(i).wait()
@@ -262,7 +275,7 @@
 
             return unused
 
-        lax.fori_loop(0, late - 1, piece, 0)
+        lax.fori_loop(0, late - 1 + extra, piece, 0)
         bring(late - 1).wait()
         multiply(w_ref.at[late - 1], SPLIT - 1, last=True)
         finish(((first + late - 1) // SPLIT) * ROWS)
@@ -274,7 +287,7 @@
     ff, width = weight.shape
     tokens = 2 * near.shape[0]
     share = tokens // parts
-    late = ff // ROWS * SPLIT - SPLIT - MORE
+    late = ff // ROWS * SPLIT - EARLY - MORE
     outs = pl.pallas_call(
         functools.partial(hidden_grad_kernel, n, parts),
         out_shape=(
@@ -299,17 +312,24 @@
 
 
 def weight_grad_kernel(sizes, hidden_ref, g_ref, out_ref, buf, sems):
-    copies = []
-    at = 0
-    for i, size in enumerate(sizes):
-        rows = pl.ds(at, size)
-        buf[rows] = contract_rows(hidden_ref[:, rows], g_ref[...]).astype(BF16)
-        copy = pltpu.make_async_copy(buf.at[rows], out_ref.at[rows], sems.at[i])
-        copy.start()
-        copies.append(copy)
-        at += size
-    for copy in copies:
-        copy.wait()
+    size = sizes[0]
+    pair = 4
+
+    def send(i):
+        rows = pl.ds(pl.multiple_of(i * size, size), size)
+        return pltpu.make_async_copy(buf.at[rows], out_ref.at[rows], sems.at[i])
+
+    def body(i, unused):
+        for j in range(pair):
+            at = i * pair + j
+            rows = pl.ds(pl.multiple_of(at * size, size), size)
+            buf[rows] = contract_rows(hidden_ref[:, rows], g_ref[...]).astype(BF16)
+            send(at).start()
+        return unused
+
+    lax.fori_loop(0, len(sizes) // pair, body, 0)
+    for i in range(len(sizes)):
+        send(i).wait()
 
 
 def weight_grad_call(hidden, g):
@@ -375,7 +395,7 @@
     def local(grad_out, pre_act, weight):
         ff, width = weight.shape
         small = power_of_two(n) and power_of_two(parts) and parts < n <= 8
-        fits = ff % ROWS == 0 and ff >= 2 * ROWS and ff % (BLOCKS * 128) == 0 and width % (SPLIT * SIDE) == 0
+        fits = ff % ROWS == 0 and ff >= 3 * ROWS and ff % (BLOCKS * 128) == 0 and width % (SPLIT * SIDE) == 0
         if small and fits and ff * width * 2 <= 40 * 2**20:
             return ring(n, parts, grad_out, pre_act, weight)
         return plain(grad_out, pre_act, weight)

time: 40.9 us -> 40.2 us (0.983)
  waiting for transfers between devices: 1.5 us -> 1.02 us
    pallas_call x1, Pallas kernels: 2.41 us -> 1.42 us  [fetch_call(): pl.pallas_call(fetch_kernel, out_shape=jax.ShapeDtypeStruct((MORE, ROWS,...]
    ppermute x7, waiting for transfers between devices: 1.5 us -> 1.02 us  [swap(): return lax.ppermute(value, axis, [(i, i ^ k) for i in range(size)])]
    pallas_call x1, Pallas kernels: 4.1 us -> 4.58 us  [gelu_call(): pl.pallas_call(functools.partial(gelu_kernel, parts), out_shape=(jax.Shap...]
  transfers between devices with their start and end apart: 7 -> 7, of which waited for: 1 -> 1; matrix products, arithmetic and copies ran while one was open for 0% -> 0% of each run, Pallas kernels for 48% -> 47%
where the time goes in v6:
time: 40.2 us; the launch traced here: 40.1 us
  Pallas kernels  29 us (72%)
  starting transfers between devices  9.33 us (23%)
  waiting for transfers between devices  1.02 us (3%)
  between operations  0.72 us (2%)
    pallas_call x1, Pallas kernels, weight_grad_call(): pl.pallas_call(functools.partial(weight_grad_kernel, sizes), out_shape=ja...  13 us
    ppermute x7, starting transfers between devices, swap(): return lax.ppermute(value, axis, [(i, i ^ k) for i in range(size)])  9.33 us
    pallas_call x1, Pallas kernels, hidden_grad_call(): pl.pallas_call(functools.partial(hidden_grad_kernel, n, parts), out_shape...  9.25 us
    pallas_call x1, Pallas kernels, gelu_call(): pl.pallas_call(functools.partial(gelu_kernel, parts), out_shape=(jax.Shap...  4.58 us
    pallas_call x1, Pallas kernels, fetch_call(): pl.pallas_call(fetch_kernel, out_shape=jax.ShapeDtypeStruct((MORE, ROWS,...  1.42 us
    ppermute x7, waiting for transfers between devices, swap(): return lax.ppermute(value, axis, [(i, i ^ k) for i in range(size)])  1.02 us
  transfers between devices with their start and end apart: 7, of which 1 were waited for; matrix products, arithmetic and copies ran while one was open for 0% of the time, Pallas kernels for 47%

profile of v6, /device:TPU:0, one launch (start us, length us, event | category | flops | bytes accessed | tf_op | source)
XLA Modules:
  0.0 40.1 jit_solution(7053715222038336797)
XLA Ops:
  0.6 3.1 %collective-permute-start = (bf16[8,3072]{1,0:T(8,128)(2,1)}, bf16[8,3072]{1,0:T(8,128)(2,1)S(1)}, u32[]{:S(2)}, u32[]{:S(2)}) collective-permute-start(bf16[8,3072]{1,0:T(8,128)(2,1)} %g_hbm.1), channel_id=1, source_target_pairs={{0,8},{4,12},{8,0},{12,4},{16,24},{20,28},{24,16},{28,20},{1,9},{5... | collective-permute-start | bytes 147464 | tf_op jit(solution)/shard_map/ppermute | solution.py:373
  3.7 2.5 %collective-permute-start.2 = (bf16[8,3072]{1,0:T(8,128)(2,1)}, bf16[8,3072]{1,0:T(8,128)(2,1)S(1)}, u32[]{:S(2)}, u32[]{:S(2)}) collective-permute-start(bf16[8,3072]{1,0:T(8,128)(2,1)} %g_hbm.1), channel_id=1, source_target_pairs={{0,24},{4,28},{8,16},{12,20},{16,8},{20,12},{24,0},{28,4},{1,25},{... | collective-permute-start | bytes 147464 | tf_op jit(solution)/shard_map/ppermute | solution.py:373
  6.2 0.1 collective-permute-start.1
  6.3 4.6 %gelu.1 = (bf16[64,6144]{1,0:T(8,128)(2,1)S(1)}, f32[16,6144]{1,0:T(8,128)S(1)}, bf16[8,3072]{1,0:T(8,128)(2,1)S(1)}, bf16[7,1536,512]{2,1,0:T(8,128)(2,1)S(1)}) custom-call(bf16[64,6144]{1,0:T(8,128)(2,1)} %x_hbm.1, bf16[8,3072]{1,0:T(8,128)(2,1)} %g_hbm.1, bf16[6144,3072]{1,0:T(8,128)(2,1)} %refs_2_.1), custom_call_target="tpu_custom_call" | custom-call | flops 7864320 | bytes 12582912 | tf_op jit(solution)/shard_map/gelu/pallas_call | solution.py:113
  10.9 0.0 collective-permute-done.refs_1_
  10.9 0.0 collective-permute-done.2.refs_3_
  10.9 1.0 %collective-permute-done.1.refs_2_ = bf16[8,3072]{1,0:T(8,128)(2,1)S(1)} collective-permute-done((bf16[8,3072]{1,0:T(8,128)(2,1)}, bf16[8,3072]{1,0:T(8,128)(2,1)S(1)}, u32[]{:S(2)}, u32[]{:S(2)}) %collective-permute-start.1) | collective-permute-done | bytes 49184 | tf_op jit(solution)/shard_map/ppermute | solution.py:373
  12.0 0.1 collective-permute-start.3
  12.0 1.4 %fetch.1.refs_4_ = bf16[1,1536,512]{2,1,0:T(8,128)(2,1)S(1)} custom-call(bf16[32,3072]{1,0:T(8,128)(2,1)S(1)} %join.1.near_ref.refs_0_, bf16[6144,3072]{1,0:T(8,128)(2,1)} %refs_2_.1), custom_call_target="tpu_custom_call" | custom-call | bytes 1572864 | tf_op jit(solution)/shard_map/fetch/pallas_call | solution.py:168
  13.5 0.0 collective-permute-done.3.refs_1_
  13.5 9.3 %hidden_grad.1 = (bf16[64,3072]{1,0:T(8,128)(2,1)S(1)}, f32[16,6144]{1,0:T(8,128)S(1)}, bf16[16,6144]{1,0:T(8,128)(2,1)S(1)}, bf16[16,6144]{1,0:T(8,128)(2,1)S(1)}, bf16[16,6144]{1,0:T(8,128)(2,1)S(1)}) custom-call(bf16[32,3072]{1,0:T(8,128)(2,1)S(1)} %join.1.near_ref.refs_0_, bf16[32,3072]{1,0:T(8,128)(2,1)S(1)} %collective-permute-done.3.refs_1_, ...), custom_call_target="tpu_custom_call" | custom-call | flops 2415919104 | bytes 37748736 | tf_op jit(solution)/shard_map/hidden_grad/pallas_call | solution.py:291
  22.7 1.6 %collective-permute-start.4 = (bf16[16,6144]{1,0:T(8,128)(2,1)S(1)}, bf16[16,6144]{1,0:T(8,128)(2,1)S(1)}, u32[]{:S(2)}, u32[]{:S(2)}) collective-permute-start(bf16[16,6144]{1,0:T(8,128)(2,1)S(1)} %get-tuple-element.15), channel_id=1, source_target_pairs={{0,1},{1,0},{2,3},{3,2},{4,5},{5,4},{6,7},{7,6},{8,9},{9,8},{10,11... | collective-permute-start | bytes 589832 | tf_op jit(solution)/shard_map/ppermute | solution.py:373
  24.3 1.5 %collective-permute-start.5 = (bf16[16,6144]{1,0:T(8,128)(2,1)S(1)}, bf16[16,6144]{1,0:T(8,128)(2,1)S(1)}, u32[]{:S(2)}, u32[]{:S(2)}) collective-permute-start(bf16[16,6144]{1,0:T(8,128)(2,1)S(1)} %get-tuple-element.16), channel_id=1, source_target_pairs={{0,2},{1,3},{2,0},{3,1},{4,6},{5,7},{6,4},{7,5},{8,10},{9,11},{10,... | collective-permute-start | bytes 589832 | tf_op jit(solution)/shard_map/ppermute | solution.py:373
  25.8 0.5 %collective-permute-start.6 = (bf16[16,6144]{1,0:T(8,128)(2,1)S(1)}, bf16[16,6144]{1,0:T(8,128)(2,1)S(1)}, u32[]{:S(2)}, u32[]{:S(2)}) collective-permute-start(bf16[16,6144]{1,0:T(8,128)(2,1)S(1)} %get-tuple-element.17), channel_id=1, source_target_pairs={{0,3},{1,2},{2,1},{3,0},{4,7},{5,6},{6,5},{7,4},{8,11},{9,10},{10,... | collective-permute-start | bytes 589832 | tf_op jit(solution)/shard_map/ppermute | solution.py:373
  26.3 13.0 %weight_grad.1 = bf16[6144,3072]{1,0:T(8,128)(2,1)} custom-call(bf16[64,6144]{1,0:T(8,128)(2,1)S(1)} %get-tuple-element.18.hidden_ref, bf16[64,3072]{1,0:T(8,128)(2,1)S(1)} %get-tuple-element.19.g_ref), custom_call_target="tpu_custom_call" | custom-call | flops 2415919104 | bytes 37748736 | tf_op jit(solution)/shard_map/weight_grad/pallas_call | solution.py:339
  39.3 0.0 collective-permute-done.4.refs_0_
  39.3 0.0 collective-permute-done.5.refs_1_
  39.3 0.0 collective-permute-done.6.refs_2_
  39.3 0.8 %total.1 = bf16[16,6144]{1,0:T(8,128)(2,1)} custom-call(f32[16,6144]{1,0:T(8,128)S(1)} %get-tuple-element.13.own_ref, f32[16,6144]{1,0:T(8,128)S(1)} %get-tuple-element.14.slope_ref, bf16[16,6144]{1,0:T(8,128)(2,1)S(1)} %collective-permute-done.4.refs_0_, bf16[16,6144]{1,0:T(8,128)(2,1)S(1)} %collective-permute-done.5.refs_1_, ...), custom_call_target="tpu_custom_call" | custom-call | tf_op jit(solution)/shard_map/total/pallas_call | solution.py:361
  (1 shorter events, 0.0 us)
Async XLA Ops:
  0.6 10.3 %collective-permute-start = (bf16[8,3072]{1,0:T(8,128)(2,1)}, bf16[8,3072]{1,0:T(8,128)(2,1)S(1)}, u32[]{:S(2)}, u32[]{:S(2)}) collective-permute-start(bf16[8,3072]{1,0:T(8,128)(2,1)} %g_hbm.1), channel_id=1, source_target_pairs={{0,8},{4,12},{8,0},{12,4},{16,24},{20,28},{24,16},{28,20},{1,9},{5... | collective-permute-start | bytes 147464 | tf_op jit(solution)/shard_map/ppermute | solution.py:373
  3.7 7.2 %collective-permute-start.2 = (bf16[8,3072]{1,0:T(8,128)(2,1)}, bf16[8,3072]{1,0:T(8,128)(2,1)S(1)}, u32[]{:S(2)}, u32[]{:S(2)}) collective-permute-start(bf16[8,3072]{1,0:T(8,128)(2,1)} %g_hbm.1), channel_id=1, source_target_pairs={{0,24},{4,28},{8,16},{12,20},{16,8},{20,12},{24,0},{28,4},{1,25},{... | collective-permute-start | bytes 147464 | tf_op jit(solution)/shard_map/ppermute | solution.py:373
  6.2 5.7 %collective-permute-start.1 = (bf16[8,3072]{1,0:T(8,128)(2,1)}, bf16[8,3072]{1,0:T(8,128)(2,1)S(1)}, u32[]{:S(2)}, u32[]{:S(2)}) collective-permute-start(bf16[8,3072]{1,0:T(8,128)(2,1)} %g_hbm.1), channel_id=1, source_target_pairs={{0,16},{4,20},{8,24},{12,28},{16,0},{20,4},{24,8},{28,12},{1,17},{... | collective-permute-start | bytes 147464 | tf_op jit(solution)/shard_map/ppermute | solution.py:373
  12.0 1.5 %collective-permute-start.3 = (bf16[32,3072]{1,0:T(8,128)(2,1)S(1)}, bf16[32,3072]{1,0:T(8,128)(2,1)S(1)}, u32[]{:S(2)}, u32[]{:S(2)}) collective-permute-start(bf16[32,3072]{1,0:T(8,128)(2,1)S(1)} %join.1.near_ref.refs_0_), channel_id=1, source_target_pairs={{0,4},{4,0},{8,12},{12,8},{16,20},{20,16},{24,28},{28,24},{1,5},{5... | collective-permute-start | bytes 589832 | tf_op jit(solution)/shard_map/ppermute | solution.py:373
  22.7 16.5 %collective-permute-start.4 = (bf16[16,6144]{1,0:T(8,128)(2,1)S(1)}, bf16[16,6144]{1,0:T(8,128)(2,1)S(1)}, u32[]{:S(2)}, u32[]{:S(2)}) collective-permute-start(bf16[16,6144]{1,0:T(8,128)(2,1)S(1)} %get-tuple-element.15), channel_id=1, source_target_pairs={{0,1},{1,0},{2,3},{3,2},{4,5},{5,4},{6,7},{7,6},{8,9},{9,8},{10,11... | collective-permute-start | bytes 589832 | tf_op jit(solution)/shard_map/ppermute | solution.py:373
  24.3 15.0 %collective-permute-start.5 = (bf16[16,6144]{1,0:T(8,128)(2,1)S(1)}, bf16[16,6144]{1,0:T(8,128)(2,1)S(1)}, u32[]{:S(2)}, u32[]{:S(2)}) collective-permute-start(bf16[16,6144]{1,0:T(8,128)(2,1)S(1)} %get-tuple-element.16), channel_id=1, source_target_pairs={{0,2},{1,3},{2,0},{3,1},{4,6},{5,7},{6,4},{7,5},{8,10},{9,11},{10,... | collective-permute-start | bytes 589832 | tf_op jit(solution)/shard_map/ppermute | solution.py:373
  25.8 13.5 %collective-permute-start.6 = (bf16[16,6144]{1,0:T(8,128)(2,1)S(1)}, bf16[16,6144]{1,0:T(8,128)(2,1)S(1)}, u32[]{:S(2)}, u32[]{:S(2)}) collective-permute-start(bf16[16,6144]{1,0:T(8,128)(2,1)S(1)} %get-tuple-element.17), channel_id=1, source_target_pairs={{0,3},{1,2},{2,1},{3,0},{4,7},{5,6},{6,5},{7,4},{8,11},{9,10},{10,... | collective-permute-start | bytes 589832 | tf_op jit(solution)/shard_map/ppermute | solution.py:373

commit v7 on v6

--- a/solution.py
+++ b/solution.py
@@ -312,24 +312,17 @@
 
 
 def weight_grad_kernel(sizes, hidden_ref, g_ref, out_ref, buf, sems):
-    size = sizes[0]
-    pair = 4
-
-    def send(i):
-        rows = pl.ds(pl.multiple_of(i * size, size), size)
-        return pltpu.make_async_copy(buf.at[rows], out_ref.at[rows], sems.at[i])
-
-    def body(i, unused):
-        for j in range(pair):
-            at = i * pair + j
-            rows = pl.ds(pl.multiple_of(at * size, size), size)
-            buf[rows] = contract_rows(hidden_ref[:, rows], g_ref[...]).astype(BF16)
-            send(at).start()
-        return unused
-
-    lax.fori_loop(0, len(sizes) // pair, body, 0)
-    for i in range(len(sizes)):
-        send(i).wait()
+    copies = []
+    at = 0
+    for i, size in enumerate(sizes):
+        rows = pl.ds(at, size)
+        buf[rows] = contract_rows(hidden_ref[:, rows], g_ref[...]).astype(BF16)
+        copy = pltpu.make_async_copy(buf.at[rows], out_ref.at[rows], sems.at[i])
+        copy.start()
+        copies.append(copy)
+        at += size
+    for copy in copies:
+        copy.wait()
 
 
 def weight_grad_call(hidden, g):

time: 40.2 us -> 40.2 us (level)
  no operation moved by 1% of the time
where the time goes in v7:
time: 40.2 us; the launch traced here: 40.1 us
  Pallas kernels  29 us (72%)
  starting transfers between devices  9.33 us (23%)
  waiting for transfers between devices  1.02 us (3%)
  between operations  0.72 us (2%)
    pallas_call x1, Pallas kernels, weight_grad_call(): pl.pallas_call(functools.partial(weight_grad_kernel, sizes), out_shape=ja...  13 us
    ppermute x7, starting transfers between devices, swap(): return lax.ppermute(value, axis, [(i, i ^ k) for i in range(size)])  9.33 us
    pallas_call x1, Pallas kernels, hidden_grad_call(): pl.pallas_call(functools.partial(hidden_grad_kernel, n, parts), out_shape...  9.25 us
    pallas_call x1, Pallas kernels, gelu_call(): pl.pallas_call(functools.partial(gelu_kernel, parts), out_shape=(jax.Shap...  4.58 us
    pallas_call x1, Pallas kernels, fetch_call(): pl.pallas_call(fetch_kernel, out_shape=jax.ShapeDtypeStruct((MORE, ROWS,...  1.42 us
    ppermute x7, waiting for transfers between devices, swap(): return lax.ppermute(value, axis, [(i, i ^ k) for i in range(size)])  1.02 us
  transfers between devices with their start and end apart: 7, of which 1 were waited for; matrix products, arithmetic and copies ran while one was open for 0% of the time, Pallas kernels for 47%

profile of v7, /device:TPU:0, one launch (start us, length us, event | category | flops | bytes accessed | tf_op | source)
XLA Modules:
  0.0 40.1 jit_solution(54486730217014331)
XLA Ops:
  0.6 3.1 %collective-permute-start = (bf16[8,3072]{1,0:T(8,128)(2,1)}, bf16[8,3072]{1,0:T(8,128)(2,1)S(1)}, u32[]{:S(2)}, u32[]{:S(2)}) collective-permute-start(bf16[8,3072]{1,0:T(8,128)(2,1)} %g_hbm.1), channel_id=1, source_target_pairs={{0,8},{4,12},{8,0},{12,4},{16,24},{20,28},{24,16},{28,20},{1,9},{5... | collective-permute-start | bytes 147464 | tf_op jit(solution)/shard_map/ppermute | solution.py:366
  3.7 2.5 %collective-permute-start.2 = (bf16[8,3072]{1,0:T(8,128)(2,1)}, bf16[8,3072]{1,0:T(8,128)(2,1)S(1)}, u32[]{:S(2)}, u32[]{:S(2)}) collective-permute-start(bf16[8,3072]{1,0:T(8,128)(2,1)} %g_hbm.1), channel_id=1, source_target_pairs={{0,24},{4,28},{8,16},{12,20},{16,8},{20,12},{24,0},{28,4},{1,25},{... | collective-permute-start | bytes 147464 | tf_op jit(solution)/shard_map/ppermute | solution.py:366
  6.2 0.1 collective-permute-start.1
  6.3 4.6 %gelu.1 = (bf16[64,6144]{1,0:T(8,128)(2,1)S(1)}, f32[16,6144]{1,0:T(8,128)S(1)}, bf16[8,3072]{1,0:T(8,128)(2,1)S(1)}, bf16[7,1536,512]{2,1,0:T(8,128)(2,1)S(1)}) custom-call(bf16[64,6144]{1,0:T(8,128)(2,1)} %x_hbm.1, bf16[8,3072]{1,0:T(8,128)(2,1)} %g_hbm.1, bf16[6144,3072]{1,0:T(8,128)(2,1)} %refs_2_.1), custom_call_target="tpu_custom_call" | custom-call | flops 7864320 | bytes 12582912 | tf_op jit(solution)/shard_map/gelu/pallas_call | solution.py:113
  10.9 0.0 collective-permute-done.refs_1_
  10.9 0.0 collective-permute-done.2.refs_3_
  10.9 1.0 %collective-permute-done.1.refs_2_ = bf16[8,3072]{1,0:T(8,128)(2,1)S(1)} collective-permute-done((bf16[8,3072]{1,0:T(8,128)(2,1)}, bf16[8,3072]{1,0:T(8,128)(2,1)S(1)}, u32[]{:S(2)}, u32[]{:S(2)}) %collective-permute-start.1) | collective-permute-done | bytes 49184 | tf_op jit(solution)/shard_map/ppermute | solution.py:366
  12.0 0.1 collective-permute-start.3
  12.0 1.4 %fetch.1.refs_4_ = bf16[1,1536,512]{2,1,0:T(8,128)(2,1)S(1)} custom-call(bf16[32,3072]{1,0:T(8,128)(2,1)S(1)} %join.1.near_ref.refs_0_, bf16[6144,3072]{1,0:T(8,128)(2,1)} %refs_2_.1), custom_call_target="tpu_custom_call" | custom-call | bytes 1572864 | tf_op jit(solution)/shard_map/fetch/pallas_call | solution.py:168
  13.5 0.0 collective-permute-done.3.refs_1_
  13.5 9.3 %hidden_grad.1 = (bf16[64,3072]{1,0:T(8,128)(2,1)S(1)}, f32[16,6144]{1,0:T(8,128)S(1)}, bf16[16,6144]{1,0:T(8,128)(2,1)S(1)}, bf16[16,6144]{1,0:T(8,128)(2,1)S(1)}, bf16[16,6144]{1,0:T(8,128)(2,1)S(1)}) custom-call(bf16[32,3072]{1,0:T(8,128)(2,1)S(1)} %join.1.near_ref.refs_0_, bf16[32,3072]{1,0:T(8,128)(2,1)S(1)} %collective-permute-done.3.refs_1_, ...), custom_call_target="tpu_custom_call" | custom-call | flops 2415919104 | bytes 37748736 | tf_op jit(solution)/shard_map/hidden_grad/pallas_call | solution.py:291
  22.7 1.6 %collective-permute-start.4 = (bf16[16,6144]{1,0:T(8,128)(2,1)S(1)}, bf16[16,6144]{1,0:T(8,128)(2,1)S(1)}, u32[]{:S(2)}, u32[]{:S(2)}) collective-permute-start(bf16[16,6144]{1,0:T(8,128)(2,1)S(1)} %get-tuple-element.15), channel_id=1, source_target_pairs={{0,1},{1,0},{2,3},{3,2},{4,5},{5,4},{6,7},{7,6},{8,9},{9,8},{10,11... | collective-permute-start | bytes 589832 | tf_op jit(solution)/shard_map/ppermute | solution.py:366
  24.3 1.5 %collective-permute-start.5 = (bf16[16,6144]{1,0:T(8,128)(2,1)S(1)}, bf16[16,6144]{1,0:T(8,128)(2,1)S(1)}, u32[]{:S(2)}, u32[]{:S(2)}) collective-permute-start(bf16[16,6144]{1,0:T(8,128)(2,1)S(1)} %get-tuple-element.16), channel_id=1, source_target_pairs={{0,2},{1,3},{2,0},{3,1},{4,6},{5,7},{6,4},{7,5},{8,10},{9,11},{10,... | collective-permute-start | bytes 589832 | tf_op jit(solution)/shard_map/ppermute | solution.py:366
  25.8 0.5 %collective-permute-start.6 = (bf16[16,6144]{1,0:T(8,128)(2,1)S(1)}, bf16[16,6144]{1,0:T(8,128)(2,1)S(1)}, u32[]{:S(2)}, u32[]{:S(2)}) collective-permute-start(bf16[16,6144]{1,0:T(8,128)(2,1)S(1)} %get-tuple-element.17), channel_id=1, source_target_pairs={{0,3},{1,2},{2,1},{3,0},{4,7},{5,6},{6,5},{7,4},{8,11},{9,10},{10,... | collective-permute-start | bytes 589832 | tf_op jit(solution)/shard_map/ppermute | solution.py:366
  26.3 13.0 %weight_grad.1 = bf16[6144,3072]{1,0:T(8,128)(2,1)} custom-call(bf16[64,6144]{1,0:T(8,128)(2,1)S(1)} %get-tuple-element.18.hidden_ref, bf16[64,3072]{1,0:T(8,128)(2,1)S(1)} %get-tuple-element.19.g_ref), custom_call_target="tpu_custom_call" | custom-call | flops 2415919104 | bytes 37748736 | tf_op jit(solution)/shard_map/weight_grad/pallas_call | solution.py:332
  39.3 0.0 collective-permute-done.4.refs_0_
  39.3 0.0 collective-permute-done.5.refs_1_
  39.3 0.0 collective-permute-done.6.refs_2_
  39.3 0.8 %total.1 = bf16[16,6144]{1,0:T(8,128)(2,1)} custom-call(f32[16,6144]{1,0:T(8,128)S(1)} %get-tuple-element.13.own_ref, f32[16,6144]{1,0:T(8,128)S(1)} %get-tuple-element.14.slope_ref, bf16[16,6144]{1,0:T(8,128)(2,1)S(1)} %collective-permute-done.4.refs_0_, bf16[16,6144]{1,0:T(8,128)(2,1)S(1)} %collective-permute-done.5.refs_1_, ...), custom_call_target="tpu_custom_call" | custom-call | tf_op jit(solution)/shard_map/total/pallas_call | solution.py:354
  (1 shorter events, 0.0 us)
Async XLA Ops:
  0.6 10.3 %collective-permute-start = (bf16[8,3072]{1,0:T(8,128)(2,1)}, bf16[8,3072]{1,0:T(8,128)(2,1)S(1)}, u32[]{:S(2)}, u32[]{:S(2)}) collective-permute-start(bf16[8,3072]{1,0:T(8,128)(2,1)} %g_hbm.1), channel_id=1, source_target_pairs={{0,8},{4,12},{8,0},{12,4},{16,24},{20,28},{24,16},{28,20},{1,9},{5... | collective-permute-start | bytes 147464 | tf_op jit(solution)/shard_map/ppermute | solution.py:366
  3.7 7.2 %collective-permute-start.2 = (bf16[8,3072]{1,0:T(8,128)(2,1)}, bf16[8,3072]{1,0:T(8,128)(2,1)S(1)}, u32[]{:S(2)}, u32[]{:S(2)}) collective-permute-start(bf16[8,3072]{1,0:T(8,128)(2,1)} %g_hbm.1), channel_id=1, source_target_pairs={{0,24},{4,28},{8,16},{12,20},{16,8},{20,12},{24,0},{28,4},{1,25},{... | collective-permute-start | bytes 147464 | tf_op jit(solution)/shard_map/ppermute | solution.py:366
  6.2 5.7 %collective-permute-start.1 = (bf16[8,3072]{1,0:T(8,128)(2,1)}, bf16[8,3072]{1,0:T(8,128)(2,1)S(1)}, u32[]{:S(2)}, u32[]{:S(2)}) collective-permute-start(bf16[8,3072]{1,0:T(8,128)(2,1)} %g_hbm.1), channel_id=1, source_target_pairs={{0,16},{4,20},{8,24},{12,28},{16,0},{20,4},{24,8},{28,12},{1,17},{... | collective-permute-start | bytes 147464 | tf_op jit(solution)/shard_map/ppermute | solution.py:366
  12.0 1.5 %collective-permute-start.3 = (bf16[32,3072]{1,0:T(8,128)(2,1)S(1)}, bf16[32,3072]{1,0:T(8,128)(2,1)S(1)}, u32[]{:S(2)}, u32[]{:S(2)}) collective-permute-start(bf16[32,3072]{1,0:T(8,128)(2,1)S(1)} %join.1.near_ref.refs_0_), channel_id=1, source_target_pairs={{0,4},{4,0},{8,12},{12,8},{16,20},{20,16},{24,28},{28,24},{1,5},{5... | collective-permute-start | bytes 589832 | tf_op jit(solution)/shard_map/ppermute | solution.py:366
  22.7 16.5 %collective-permute-start.4 = (bf16[16,6144]{1,0:T(8,128)(2,1)S(1)}, bf16[16,6144]{1,0:T(8,128)(2,1)S(1)}, u32[]{:S(2)}, u32[]{:S(2)}) collective-permute-start(bf16[16,6144]{1,0:T(8,128)(2,1)S(1)} %get-tuple-element.15), channel_id=1, source_target_pairs={{0,1},{1,0},{2,3},{3,2},{4,5},{5,4},{6,7},{7,6},{8,9},{9,8},{10,11... | collective-permute-start | bytes 589832 | tf_op jit(solution)/shard_map/ppermute | solution.py:366
  24.3 15.0 %collective-permute-start.5 = (bf16[16,6144]{1,0:T(8,128)(2,1)S(1)}, bf16[16,6144]{1,0:T(8,128)(2,1)S(1)}, u32[]{:S(2)}, u32[]{:S(2)}) collective-permute-start(bf16[16,6144]{1,0:T(8,128)(2,1)S(1)} %get-tuple-element.16), channel_id=1, source_target_pairs={{0,2},{1,3},{2,0},{3,1},{4,6},{5,7},{6,4},{7,5},{8,10},{9,11},{10,... | collective-permute-start | bytes 589832 | tf_op jit(solution)/shard_map/ppermute | solution.py:366
  25.8 13.5 %collective-permute-start.6 = (bf16[16,6144]{1,0:T(8,128)(2,1)S(1)}, bf16[16,6144]{1,0:T(8,128)(2,1)S(1)}, u32[]{:S(2)}, u32[]{:S(2)}) collective-permute-start(bf16[16,6144]{1,0:T(8,128)(2,1)S(1)} %get-tuple-element.17), channel_id=1, source_target_pairs={{0,3},{1,2},{2,1},{3,0},{4,7},{5,6},{6,5},{7,4},{8,11},{9,10},{10,... | collective-permute-start | bytes 589832 | tf_op jit(solution)/shard_map/ppermute | solution.py:366
